TPU v7x, 256 devices: a whole 4x4x8 slice. The times are simulated.
256 devices in a mesh: depth: 8 (over x, core), rows: 32 (over z, y).
Axes of the slice: x: 4, y: 4, z: 8, core: 2. Of those that a mesh axis runs over, the one named last changes fastest.
Arguments:
- source_top: bfloat16 [2, 2, 512, 512], P(None, None, 'rows'), may hold values from -8 to 8
- adjoint_bottom: bfloat16 [2, 2, 512, 512], P(None, None, 'rows'), may hold values from -8 to 8
- slowness: float32 [8, 512, 512], P('depth', 'rows'), may hold values from 0.7 to 1.3
- correction: float32 [8, 512, 512], P('depth', 'rows'), may hold values from -0.16 to 0.16
- slowness_ref: float32 [8], P('depth'), may hold values from 0.9 to 1.1
- omega: float32 [2], replicated, may hold values from 0.8 to 1.6
Outputs:
- gradient: float32 [8, 512, 512], P('depth', 'rows')
All inputs are finite; a program needn't handle non-finite values.
Results may differ from a plain program's by a relative error of at most 0.025.
Values may be sent and summed in bfloat16 or wider, within the bound.
A program may use at most 64 MiB of HBM per device.

v0:
```python
from functools import partial
import math

import jax
import jax.numpy as jnp
from jax import lax
from jax.sharding import PartitionSpec as P

depth_step = 1.0
y_radix = 16


def extended_2(shard, sides, width):
    for axis, dim in sides:
        size, length = (lax.axis_size(axis), shard.shape[dim])
        up = [(i, (i + 1) % size) for i in range(size)]
        down = [(j, i) for i, j in up]
        last = lax.slice_in_dim(shard, length - width, length, axis=dim)
        initial = lax.slice_in_dim(shard, 0, width, axis=dim)
        before = lax.ppermute(last, axis, up)
        after = lax.ppermute(initial, axis, down)
        shard = jnp.concatenate([before, shard, after], axis=dim)
    return shard


def passed_along(shard, axis, by):
    length = lax.axis_size(axis)
    pairs = [(i, i + by) for i in range(length) if 0 <= i + by < length]
    return lax.ppermute(shard, axis, pairs)


def from_behind(block, axis, distance):
    devices = range(lax.axis_size(axis))
    route = [((i - distance) % len(devices), i) for i in devices]
    return lax.ppermute(block, axis, route)


def dft_table(length, direction):
    row_index = lax.broadcasted_iota(jnp.int32, (length, length), 0)
    col_index = lax.broadcasted_iota(jnp.int32, (length, length), 1)
    angles = (row_index * col_index % length).astype(jnp.float32) * (2.0 * math.pi / length)
    norm_scale = 1.0 / math.sqrt(length)
    return (jnp.cos(angles) * norm_scale, direction * jnp.sin(angles) * norm_scale)


def twiddle_table(first_len, second_len, length, direction):
    row_index = lax.broadcasted_iota(jnp.int32, (first_len, second_len), 0)
    col_index = lax.broadcasted_iota(jnp.int32, (first_len, second_len), 1)
    angles = (row_index * col_index % length).astype(jnp.float32) * (2.0 * math.pi / length)
    return (jnp.cos(angles), direction * jnp.sin(angles))


def contract(pattern, values, matrix):
    product = partial(
        jnp.einsum, pattern, precision=lax.Precision.HIGHEST, preferred_element_type=jnp.float32
    )
    return (
        product(values[0], matrix[0]) - product(values[1], matrix[1]),
        product(values[0], matrix[1]) + product(values[1], matrix[0]),
    )


def rotate(values, factor):
    return (
        values[0] * factor[0] - values[1] * factor[1],
        values[0] * factor[1] + values[1] * factor[0],
    )


def conjugate(values):
    return (values[0], -values[1])


def split_parts(stacked):
    return (stacked[:, 0].astype(jnp.float32), stacked[:, 1].astype(jnp.float32))


def joined_bf16(values):
    return jnp.stack(values, 1).astype(jnp.bfloat16)


def wavenumbers(positions, length):
    signed = jnp.where(positions >= length // 2, positions - length, positions)
    return signed.astype(jnp.float32) * (2.0 * math.pi / length)


def forward_rows(values):
    slot_count, rows_here, width_y = values[0].shape
    inner_len = width_y // y_radix
    shaped = tuple((member.reshape(slot_count, rows_here, y_radix, inner_len) for member in values))
    section_one = contract("kxab,ac->kxcb", shaped, dft_table(y_radix, -1.0))
    section_one = rotate(section_one, twiddle_table(y_radix, inner_len, width_y, -1.0))
    section_two = contract("kxcb,bd->kxcd", section_one, dft_table(inner_len, -1.0))
    return tuple((member.reshape(slot_count, rows_here, width_y) for member in section_two))


def inverse_rows(values):
    slot_count, rows_here, width_y = values[0].shape
    inner_len = width_y // y_radix
    shaped = tuple((member.reshape(slot_count, rows_here, y_radix, inner_len) for member in values))
    section_one = contract("kxcd,bd->kxcb", shaped, dft_table(inner_len, 1.0))
    section_one = rotate(section_one, twiddle_table(y_radix, inner_len, width_y, 1.0))
    section_two = contract("kxcb,ac->kxab", section_one, dft_table(y_radix, 1.0))
    return tuple((member.reshape(slot_count, rows_here, width_y) for member in section_two))


def forward_cols(values, row_parts):
    slot_count, rows_here, width_y = values[0].shape
    local_cols = width_y // row_parts
    width_x = rows_here * row_parts
    shaped = tuple(
        (member.reshape(slot_count, rows_here, row_parts, local_cols) for member in values)
    )
    section_one = contract("kbay,ac->kbcy", shaped, dft_table(row_parts, -1.0))
    factor = twiddle_table(rows_here, row_parts, width_x, -1.0)
    section_one = rotate(section_one, (factor[0][:, :, None], factor[1][:, :, None]))
    section_two = contract("kbcy,bd->kycd", section_one, dft_table(rows_here, -1.0))
    return tuple((member.reshape(slot_count, local_cols, width_x) for member in section_two))


def inverse_cols(values, row_parts):
    slot_count, local_cols, width_x = values[0].shape
    rows_here = width_x // row_parts
    shaped = tuple(
        (member.reshape(slot_count, local_cols, row_parts, rows_here) for member in values)
    )
    section_one = contract("kycd,bd->kbcy", shaped, dft_table(rows_here, 1.0))
    factor = twiddle_table(rows_here, row_parts, width_x, 1.0)
    section_one = rotate(section_one, (factor[0][:, :, None], factor[1][:, :, None]))
    section_two = contract("kbcy,ac->kbay", section_one, dft_table(row_parts, 1.0))
    return tuple(
        (member.reshape(slot_count, rows_here, row_parts * local_cols) for member in section_two)
    )


def rim_laplace(rimmed):
    widened_values = rimmed.astype(jnp.float32)
    center = widened_values[:, :, 1:-1]
    return (
        widened_values[:, :, 2:]
        + widened_values[:, :, :-2]
        + jnp.roll(center, 1, 3)
        + jnp.roll(center, -1, 3)
        - 4.0 * center
    )


def per_device(source_top, adjoint_bottom, slowness, correction, slowness_ref, omega):
    row_parts = lax.axis_size("rows")
    section_count = lax.axis_size("depth")
    section_id = lax.axis_index("depth")
    part_id = lax.axis_index("rows")
    freq_count = omega.shape[0]
    rows_here = slowness.shape[1]
    width_y = slowness.shape[2]
    width_x = rows_here * row_parts
    local_cols = width_y // row_parts
    slot_count = 1
    group_count = freq_count // slot_count
    tick_count = group_count + section_count
    slow_here = slowness[0]
    coef_here = correction[0]
    ref_here = slowness_ref[0]
    inner_y = width_y // y_radix
    spectral_y = part_id * local_cols + lax.iota(jnp.int32, local_cols)
    index_y = spectral_y // inner_y + y_radix * (spectral_y % inner_y)
    first_x = lax.broadcasted_iota(jnp.int32, (row_parts, rows_here), 0)
    second_x = lax.broadcasted_iota(jnp.int32, (row_parts, rows_here), 1)
    index_x = (first_x + row_parts * second_x).reshape(width_x)
    wave_y = wavenumbers(index_y, width_y)
    wave_x = wavenumbers(index_x, width_x)

    def phase_for(omega_slot):
        squared = (
            (omega_slot[:, None, None] * ref_here) ** 2
            - wave_x[None, None, :] ** 2
            - wave_y[None, :, None] ** 2
        )
        damping = jnp.exp(-jnp.sqrt(jnp.maximum(-squared, 0.0)) * depth_step)
        angles = jnp.sqrt(jnp.maximum(squared, 0.0)) * depth_step
        return (damping * jnp.cos(angles), damping * jnp.sin(angles))

    def lens_for(omega_slot, slow_rows):
        angles = omega_slot[:, None, None] * (slow_rows - ref_here) * depth_step
        return (jnp.cos(angles), jnp.sin(angles))

    def slot_of(source_array, group_id):
        start_row = jnp.clip(group_id, 0, group_count - 1) * slot_count
        return lax.dynamic_slice_in_dim(source_array, start_row, slot_count, 0)

    def store_slot(buffer, values, group_id):
        start_row = jnp.clip(group_id, 0, group_count - 1) * slot_count
        active = jnp.logical_and(group_id >= 0, group_id < group_count)
        old_slot = lax.dynamic_slice_in_dim(buffer, start_row, slot_count, 0)
        return lax.dynamic_update_slice_in_dim(
            buffer, jnp.where(active, values, old_slot), start_row, 0
        )

    def one_tick(tick_index, loop_state):
        fwd_in, adj_in, fwd_store, adj_store = loop_state
        group_f = tick_index - section_id
        group_a = tick_index - section_count + section_id
        omega_f = slot_of(omega, group_f)
        omega_a = slot_of(omega, group_a)
        adj_center = adj_in[:, :, 1:-1].astype(jnp.float32)
        adj_laplace = rim_laplace(adj_in)
        pulled = (
            adj_center[:, 0] + coef_here * adj_laplace[:, 1],
            adj_center[:, 1] - coef_here * adj_laplace[:, 0],
        )
        pulled = rotate(pulled, conjugate(lens_for(omega_a, slow_here)))
        spec_f = forward_rows(split_parts(fwd_in))
        spec_a = forward_rows(pulled)
        cross_f, cross_a = (
            lax.all_to_all(joined_bf16(spec_f), "rows", split_axis=3, concat_axis=3, tiled=True),
            lax.all_to_all(joined_bf16(spec_a), "rows", split_axis=3, concat_axis=3, tiled=True),
        )
        wave_f = rotate(forward_cols(split_parts(cross_f), row_parts), phase_for(omega_f))
        wave_a = rotate(
            forward_cols(split_parts(cross_a), row_parts), conjugate(phase_for(omega_a))
        )
        outgoing = (
            joined_bf16(inverse_cols(wave_f, row_parts)),
            joined_bf16(inverse_cols(wave_a, row_parts)),
        )
        back_f, back_a = (
            lax.all_to_all(outgoing[0], "rows", split_axis=3, concat_axis=3, tiled=True),
            lax.all_to_all(outgoing[1], "rows", split_axis=3, concat_axis=3, tiled=True),
        )
        field_f = inverse_rows(split_parts(back_f))
        field_a = joined_bf16(inverse_rows(split_parts(back_a)))
        lensed = rotate(field_f, lens_for(omega_f, slow_here))
        scaled = joined_bf16((coef_here * lensed[0], coef_here * lensed[1]))
        upward = jnp.where(section_id == 0, slot_of(adjoint_bottom, tick_index), field_a)
        scaled_rims, upward_rims = (
            extended_2(scaled, (("rows", 2),), 1),
            extended_2(upward, (("rows", 2),), 1),
        )
        fwd_laplace = rim_laplace(scaled_rims)
        fwd_out = joined_bf16((lensed[0] - fwd_laplace[:, 1], lensed[1] + fwd_laplace[:, 0]))
        passed = passed_along(fwd_out, "depth", 1)
        next_up = from_behind(upward_rims, "depth", -1)
        next_fwd = jnp.where(section_id == 0, slot_of(source_top, tick_index + 1), passed)
        fwd_store = store_slot(fwd_store, fwd_out, group_f)
        adj_store = store_slot(adj_store, adj_in[:, :, 1:-1], group_a)
        return (next_fwd, next_up, fwd_store, adj_store)

    initial = (
        slot_of(source_top, 0),
        jnp.zeros((slot_count, 2, rows_here + 2, width_y), jnp.bfloat16),
        jnp.zeros((freq_count, 2, rows_here, width_y), jnp.bfloat16),
        jnp.zeros((freq_count, 2, rows_here, width_y), jnp.bfloat16),
    )
    final_state = lax.fori_loop(0, tick_count, one_tick, initial)
    forward_part = split_parts(final_state[2])
    adjoint_part = split_parts(final_state[3])
    product = forward_part[0] * adjoint_part[1] - forward_part[1] * adjoint_part[0]
    gradient = jnp.sum(omega[:, None, None] * product, axis=0)
    return gradient[None]


def solution(mesh):
    in_specs = (
        P(None, None, "rows", None),
        P(None, None, "rows", None),
        P("depth", "rows", None),
        P("depth", "rows", None),
        P("depth"),
        P(),
    )
    out_specs = P("depth", "rows", None)
    return jax.shard_map(
        per_device, mesh=mesh, in_specs=in_specs, out_specs=out_specs, check_vma=False
    )
```

profile of v0, /device:TPU:32, one launch (start us, length us, event | category | flops | bytes accessed | tf_op | source)
XLA Modules:
  0.0 1052.2 jit_solution(1982745217700264642)
XLA Ops:
  1.7 1049.9 %while.24 = (s32[]{:T(128)}, bf16[1,2,16,512]{3,2,1,0:T(8,128)(2,1)S(1)}, bf16[1,2,18,512]{3,2,1,0:T(8,128)(2,1)S(1)}, bf16[2,2,16,512]{3,2,1,0:T(8,128)(2,1)S(1...) while((s32[]{:T(128)}, ...), condition=%wide.region_1.2_spmd.clone.clone, body=%wide.region_0.1_spmd.clone.clone.sunk | while | flops 154105296 | bytes 13749523 | solution.py:254
  9.0 11.4 %all-to-all-start = ((bf16[32,2,256]{2,1,0:T(2,128)(2,1)}), bf16[32,2,256]{2,1,0:T(2,128)(2,1)S(1)}, u32[]{:S(2)}, u32[]{:S(2)}) async-start(bf16[32,2,256]{2,1,0:T(2,128)(2,1)} %reshape.2423), calls=%async_computation | async-start | bytes 65536 | tf_op jit(solution)/shard_map/while/body/eval_jaxpr/all_to_all | solution.py:216
  29.0 8.3 all-to-all-start.1
  39.5 6.5 all-to-all-done.1
  68.5 7.0 all-to-all-done.3
  116.7 7.2 all-to-all-start
  132.6 8.3 all-to-all-start.1
  143.1 6.5 all-to-all-done.1
  172.1 7.2 all-to-all-done.3
  186.9 6.0 all-to-all-done.2
  221.3 7.4 all-to-all-start
  237.3 8.3 all-to-all-start.1
  247.8 6.5 all-to-all-done.1
  276.9 7.2 all-to-all-done.3
  291.7 6.0 all-to-all-done.2
  326.0 7.4 all-to-all-start
  342.1 8.3 all-to-all-start.1
  352.5 6.5 all-to-all-done.1
  381.6 7.2 all-to-all-done.3
  396.4 6.0 all-to-all-done.2
  430.6 7.4 all-to-all-start
  446.7 8.3 all-to-all-start.1
  457.2 6.5 all-to-all-done.1
  486.2 7.2 all-to-all-done.3
  501.0 6.0 all-to-all-done.2
  535.3 7.4 all-to-all-start
  551.3 8.3 all-to-all-start.1
  561.8 6.5 all-to-all-done.1
  590.9 7.2 all-to-all-done.3
  605.7 6.0 all-to-all-done.2
  640.0 7.4 all-to-all-start
  656.0 8.3 all-to-all-start.1
  666.5 6.5 all-to-all-done.1
  695.6 7.2 all-to-all-done.3
  744.7 7.4 all-to-all-start
  760.8 8.3 all-to-all-start.1
  771.2 6.5 all-to-all-done.1
  800.3 7.2 all-to-all-done.3
  815.1 6.0 all-to-all-done.2
  849.4 7.4 all-to-all-start
  865.5 8.3 all-to-all-start.1
  875.9 6.5 all-to-all-done.1
  905.0 7.2 all-to-all-done.3
  954.1 7.4 all-to-all-start
  970.2 8.3 all-to-all-start.1
  980.6 6.5 all-to-all-done.1
  1009.7 7.2 all-to-all-done.3
  1024.5 6.0 all-to-all-done.2
  (1869 shorter events, 676.1 us)
Async XLA Ops:
  9.0 20.0 %all-to-all-start = ((bf16[32,2,256]{2,1,0:T(2,128)(2,1)}), bf16[32,2,256]{2,1,0:T(2,128)(2,1)S(1)}, u32[]{:S(2)}, u32[]{:S(2)}) async-start(bf16[32,2,256]{2,1,0:T(2,128)(2,1)} %reshape.2423), calls=%async_computation | async-start | bytes 65536 | tf_op jit(solution)/shard_map/while/body/eval_jaxpr/all_to_all | solution.py:216
  29.0 17.0 %all-to-all-start.1 = ((bf16[32,2,256]{2,1,0:T(2,128)(2,1)}), bf16[32,2,256]{2,1,0:T(2,128)(2,1)S(1)}, u32[]{:S(2)}, u32[]{:S(2)}) async-start(bf16[32,2,256]{2,1,0:T(2,128)(2,1)} %reshape.2427), calls=%async_computation.1 | async-start | bytes 65536 | tf_op jit(solution)/shard_map/while/body/eval_jaxpr/all_to_all | solution.py:215
  61.9 13.7 %all-to-all-start.3 = ((bf16[32,2,256]{2,1,0:T(2,128)(2,1)}), bf16[32,2,256]{2,1,0:T(2,128)(2,1)S(1)}, u32[]{:S(2)}, u32[]{:S(2)}) async-start(bf16[32,2,256]{2,1,0:T(2,128)(2,1)} %reshape.2437), calls=%async_computation.3 | async-start | bytes 65536 | tf_op jit(solution)/shard_map/while/body/eval_jaxpr/all_to_all | solution.py:228
  75.6 13.7 %all-to-all-start.2 = ((bf16[32,2,256]{2,1,0:T(2,128)(2,1)}), bf16[32,2,256]{2,1,0:T(2,128)(2,1)S(1)}, u32[]{:S(2)}, u32[]{:S(2)}) async-start(bf16[32,2,256]{2,1,0:T(2,128)(2,1)} %reshape.2429), calls=%async_computation.2 | async-start | bytes 65536 | tf_op jit(solution)/shard_map/while/body/eval_jaxpr/all_to_all | solution.py:227
  97.7 8.5 collective-permute-start.3
  116.7 15.9 %all-to-all-start = ((bf16[32,2,256]{2,1,0:T(2,128)(2,1)}), bf16[32,2,256]{2,1,0:T(2,128)(2,1)S(1)}, u32[]{:S(2)}, u32[]{:S(2)}) async-start(bf16[32,2,256]{2,1,0:T(2,128)(2,1)} %reshape.2423), calls=%async_computation | async-start | bytes 65536 | tf_op jit(solution)/shard_map/while/body/eval_jaxpr/all_to_all | solution.py:216
  132.6 17.0 %all-to-all-start.1 = ((bf16[32,2,256]{2,1,0:T(2,128)(2,1)}), bf16[32,2,256]{2,1,0:T(2,128)(2,1)S(1)}, u32[]{:S(2)}, u32[]{:S(2)}) async-start(bf16[32,2,256]{2,1,0:T(2,128)(2,1)} %reshape.2427), calls=%async_computation.1 | async-start | bytes 65536 | tf_op jit(solution)/shard_map/while/body/eval_jaxpr/all_to_all | solution.py:215
  165.5 13.8 %all-to-all-start.3 = ((bf16[32,2,256]{2,1,0:T(2,128)(2,1)}), bf16[32,2,256]{2,1,0:T(2,128)(2,1)S(1)}, u32[]{:S(2)}, u32[]{:S(2)}) async-start(bf16[32,2,256]{2,1,0:T(2,128)(2,1)} %reshape.2437), calls=%async_computation.3 | async-start | bytes 65536 | tf_op jit(solution)/shard_map/while/body/eval_jaxpr/all_to_all | solution.py:228
  179.3 13.7 %all-to-all-start.2 = ((bf16[32,2,256]{2,1,0:T(2,128)(2,1)}), bf16[32,2,256]{2,1,0:T(2,128)(2,1)S(1)}, u32[]{:S(2)}, u32[]{:S(2)}) async-start(bf16[32,2,256]{2,1,0:T(2,128)(2,1)} %reshape.2429), calls=%async_computation.2 | async-start | bytes 65536 | tf_op jit(solution)/shard_map/while/body/eval_jaxpr/all_to_all | solution.py:227
  201.3 8.5 collective-permute-start.3
  221.3 16.1 %all-to-all-start = ((bf16[32,2,256]{2,1,0:T(2,128)(2,1)}), bf16[32,2,256]{2,1,0:T(2,128)(2,1)S(1)}, u32[]{:S(2)}, u32[]{:S(2)}) async-start(bf16[32,2,256]{2,1,0:T(2,128)(2,1)} %reshape.2423), calls=%async_computation | async-start | bytes 65536 | tf_op jit(solution)/shard_map/while/body/eval_jaxpr/all_to_all | solution.py:216
  237.3 17.0 %all-to-all-start.1 = ((bf16[32,2,256]{2,1,0:T(2,128)(2,1)}), bf16[32,2,256]{2,1,0:T(2,128)(2,1)S(1)}, u32[]{:S(2)}, u32[]{:S(2)}) async-start(bf16[32,2,256]{2,1,0:T(2,128)(2,1)} %reshape.2427), calls=%async_computation.1 | async-start | bytes 65536 | tf_op jit(solution)/shard_map/while/body/eval_jaxpr/all_to_all | solution.py:215
  270.2 13.8 %all-to-all-start.3 = ((bf16[32,2,256]{2,1,0:T(2,128)(2,1)}), bf16[32,2,256]{2,1,0:T(2,128)(2,1)S(1)}, u32[]{:S(2)}, u32[]{:S(2)}) async-start(bf16[32,2,256]{2,1,0:T(2,128)(2,1)} %reshape.2437), calls=%async_computation.3 | async-start | bytes 65536 | tf_op jit(solution)/shard_map/while/body/eval_jaxpr/all_to_all | solution.py:228
  284.1 13.7 %all-to-all-start.2 = ((bf16[32,2,256]{2,1,0:T(2,128)(2,1)}), bf16[32,2,256]{2,1,0:T(2,128)(2,1)S(1)}, u32[]{:S(2)}, u32[]{:S(2)}) async-start(bf16[32,2,256]{2,1,0:T(2,128)(2,1)} %reshape.2429), calls=%async_computation.2 | async-start | bytes 65536 | tf_op jit(solution)/shard_map/while/body/eval_jaxpr/all_to_all | solution.py:227
  306.1 8.5 collective-permute-start.3
  326.0 16.1 %all-to-all-start = ((bf16[32,2,256]{2,1,0:T(2,128)(2,1)}), bf16[32,2,256]{2,1,0:T(2,128)(2,1)S(1)}, u32[]{:S(2)}, u32[]{:S(2)}) async-start(bf16[32,2,256]{2,1,0:T(2,128)(2,1)} %reshape.2423), calls=%async_computation | async-start | bytes 65536 | tf_op jit(solution)/shard_map/while/body/eval_jaxpr/all_to_all | solution.py:216
  342.1 17.0 %all-to-all-start.1 = ((bf16[32,2,256]{2,1,0:T(2,128)(2,1)}), bf16[32,2,256]{2,1,0:T(2,128)(2,1)S(1)}, u32[]{:S(2)}, u32[]{:S(2)}) async-start(bf16[32,2,256]{2,1,0:T(2,128)(2,1)} %reshape.2427), calls=%async_computation.1 | async-start | bytes 65536 | tf_op jit(solution)/shard_map/while/body/eval_jaxpr/all_to_all | solution.py:215
  374.9 13.8 %all-to-all-start.3 = ((bf16[32,2,256]{2,1,0:T(2,128)(2,1)}), bf16[32,2,256]{2,1,0:T(2,128)(2,1)S(1)}, u32[]{:S(2)}, u32[]{:S(2)}) async-start(bf16[32,2,256]{2,1,0:T(2,128)(2,1)} %reshape.2437), calls=%async_computation.3 | async-start | bytes 65536 | tf_op jit(solution)/shard_map/while/body/eval_jaxpr/all_to_all | solution.py:228
  388.8 13.7 %all-to-all-start.2 = ((bf16[32,2,256]{2,1,0:T(2,128)(2,1)}), bf16[32,2,256]{2,1,0:T(2,128)(2,1)S(1)}, u32[]{:S(2)}, u32[]{:S(2)}) async-start(bf16[32,2,256]{2,1,0:T(2,128)(2,1)} %reshape.2429), calls=%async_computation.2 | async-start | bytes 65536 | tf_op jit(solution)/shard_map/while/body/eval_jaxpr/all_to_all | solution.py:227
  410.8 8.5 collective-permute-start.3
  430.6 16.1 %all-to-all-start = ((bf16[32,2,256]{2,1,0:T(2,128)(2,1)}), bf16[32,2,256]{2,1,0:T(2,128)(2,1)S(1)}, u32[]{:S(2)}, u32[]{:S(2)}) async-start(bf16[32,2,256]{2,1,0:T(2,128)(2,1)} %reshape.2423), calls=%async_computation | async-start | bytes 65536 | tf_op jit(solution)/shard_map/while/body/eval_jaxpr/all_to_all | solution.py:216
  446.7 17.0 %all-to-all-start.1 = ((bf16[32,2,256]{2,1,0:T(2,128)(2,1)}), bf16[32,2,256]{2,1,0:T(2,128)(2,1)S(1)}, u32[]{:S(2)}, u32[]{:S(2)}) async-start(bf16[32,2,256]{2,1,0:T(2,128)(2,1)} %reshape.2427), calls=%async_computation.1 | async-start | bytes 65536 | tf_op jit(solution)/shard_map/while/body/eval_jaxpr/all_to_all | solution.py:215
  479.6 13.8 %all-to-all-start.3 = ((bf16[32,2,256]{2,1,0:T(2,128)(2,1)}), bf16[32,2,256]{2,1,0:T(2,128)(2,1)S(1)}, u32[]{:S(2)}, u32[]{:S(2)}) async-start(bf16[32,2,256]{2,1,0:T(2,128)(2,1)} %reshape.2437), calls=%async_computation.3 | async-start | bytes 65536 | tf_op jit(solution)/shard_map/while/body/eval_jaxpr/all_to_all | solution.py:228
  493.4 13.7 %all-to-all-start.2 = ((bf16[32,2,256]{2,1,0:T(2,128)(2,1)}), bf16[32,2,256]{2,1,0:T(2,128)(2,1)S(1)}, u32[]{:S(2)}, u32[]{:S(2)}) async-start(bf16[32,2,256]{2,1,0:T(2,128)(2,1)} %reshape.2429), calls=%async_computation.2 | async-start | bytes 65536 | tf_op jit(solution)/shard_map/while/body/eval_jaxpr/all_to_all | solution.py:227
  515.4 8.5 collective-permute-start.3
  535.3 16.1 %all-to-all-start = ((bf16[32,2,256]{2,1,0:T(2,128)(2,1)}), bf16[32,2,256]{2,1,0:T(2,128)(2,1)S(1)}, u32[]{:S(2)}, u32[]{:S(2)}) async-start(bf16[32,2,256]{2,1,0:T(2,128)(2,1)} %reshape.2423), calls=%async_computation | async-start | bytes 65536 | tf_op jit(solution)/shard_map/while/body/eval_jaxpr/all_to_all | solution.py:216
  551.3 17.0 %all-to-all-start.1 = ((bf16[32,2,256]{2,1,0:T(2,128)(2,1)}), bf16[32,2,256]{2,1,0:T(2,128)(2,1)S(1)}, u32[]{:S(2)}, u32[]{:S(2)}) async-start(bf16[32,2,256]{2,1,0:T(2,128)(2,1)} %reshape.2427), calls=%async_computation.1 | async-start | bytes 65536 | tf_op jit(solution)/shard_map/while/body/eval_jaxpr/all_to_all | solution.py:215
  584.2 13.8 %all-to-all-start.3 = ((bf16[32,2,256]{2,1,0:T(2,128)(2,1)}), bf16[32,2,256]{2,1,0:T(2,128)(2,1)S(1)}, u32[]{:S(2)}, u32[]{:S(2)}) async-start(bf16[32,2,256]{2,1,0:T(2,128)(2,1)} %reshape.2437), calls=%async_computation.3 | async-start | bytes 65536 | tf_op jit(solution)/shard_map/while/body/eval_jaxpr/all_to_all | solution.py:228
  598.1 13.7 %all-to-all-start.2 = ((bf16[32,2,256]{2,1,0:T(2,128)(2,1)}), bf16[32,2,256]{2,1,0:T(2,128)(2,1)S(1)}, u32[]{:S(2)}, u32[]{:S(2)}) async-start(bf16[32,2,256]{2,1,0:T(2,128)(2,1)} %reshape.2429), calls=%async_computation.2 | async-start | bytes 65536 | tf_op jit(solution)/shard_map/while/body/eval_jaxpr/all_to_all | solution.py:227
  620.1 8.5 collective-permute-start.3
  640.0 16.1 %all-to-all-start = ((bf16[32,2,256]{2,1,0:T(2,128)(2,1)}), bf16[32,2,256]{2,1,0:T(2,128)(2,1)S(1)}, u32[]{:S(2)}, u32[]{:S(2)}) async-start(bf16[32,2,256]{2,1,0:T(2,128)(2,1)} %reshape.2423), calls=%async_computation | async-start | bytes 65536 | tf_op jit(solution)/shard_map/while/body/eval_jaxpr/all_to_all | solution.py:216
  656.0 17.0 %all-to-all-start.1 = ((bf16[32,2,256]{2,1,0:T(2,128)(2,1)}), bf16[32,2,256]{2,1,0:T(2,128)(2,1)S(1)}, u32[]{:S(2)}, u32[]{:S(2)}) async-start(bf16[32,2,256]{2,1,0:T(2,128)(2,1)} %reshape.2427), calls=%async_computation.1 | async-start | bytes 65536 | tf_op jit(solution)/shard_map/while/body/eval_jaxpr/all_to_all | solution.py:215
  688.9 13.8 %all-to-all-start.3 = ((bf16[32,2,256]{2,1,0:T(2,128)(2,1)}), bf16[32,2,256]{2,1,0:T(2,128)(2,1)S(1)}, u32[]{:S(2)}, u32[]{:S(2)}) async-start(bf16[32,2,256]{2,1,0:T(2,128)(2,1)} %reshape.2437), calls=%async_computation.3 | async-start | bytes 65536 | tf_op jit(solution)/shard_map/while/body/eval_jaxpr/all_to_all | solution.py:228
  702.8 13.7 %all-to-all-start.2 = ((bf16[32,2,256]{2,1,0:T(2,128)(2,1)}), bf16[32,2,256]{2,1,0:T(2,128)(2,1)S(1)}, u32[]{:S(2)}, u32[]{:S(2)}) async-start(bf16[32,2,256]{2,1,0:T(2,128)(2,1)} %reshape.2429), calls=%async_computation.2 | async-start | bytes 65536 | tf_op jit(solution)/shard_map/while/body/eval_jaxpr/all_to_all | solution.py:227
  724.8 8.5 collective-permute-start.3
  744.7 16.1 %all-to-all-start = ((bf16[32,2,256]{2,1,0:T(2,128)(2,1)}), bf16[32,2,256]{2,1,0:T(2,128)(2,1)S(1)}, u32[]{:S(2)}, u32[]{:S(2)}) async-start(bf16[32,2,256]{2,1,0:T(2,128)(2,1)} %reshape.2423), calls=%async_computation | async-start | bytes 65536 | tf_op jit(solution)/shard_map/while/body/eval_jaxpr/all_to_all | solution.py:216
  760.8 17.0 %all-to-all-start.1 = ((bf16[32,2,256]{2,1,0:T(2,128)(2,1)}), bf16[32,2,256]{2,1,0:T(2,128)(2,1)S(1)}, u32[]{:S(2)}, u32[]{:S(2)}) async-start(bf16[32,2,256]{2,1,0:T(2,128)(2,1)} %reshape.2427), calls=%async_computation.1 | async-start | bytes 65536 | tf_op jit(solution)/shard_map/while/body/eval_jaxpr/all_to_all | solution.py:215
  793.6 13.8 %all-to-all-start.3 = ((bf16[32,2,256]{2,1,0:T(2,128)(2,1)}), bf16[32,2,256]{2,1,0:T(2,128)(2,1)S(1)}, u32[]{:S(2)}, u32[]{:S(2)}) async-start(bf16[32,2,256]{2,1,0:T(2,128)(2,1)} %reshape.2437), calls=%async_computation.3 | async-start | bytes 65536 | tf_op jit(solution)/shard_map/while/body/eval_jaxpr/all_to_all | solution.py:228
  807.5 13.7 %all-to-all-start.2 = ((bf16[32,2,256]{2,1,0:T(2,128)(2,1)}), bf16[32,2,256]{2,1,0:T(2,128)(2,1)S(1)}, u32[]{:S(2)}, u32[]{:S(2)}) async-start(bf16[32,2,256]{2,1,0:T(2,128)(2,1)} %reshape.2429), calls=%async_computation.2 | async-start | bytes 65536 | tf_op jit(solution)/shard_map/while/body/eval_jaxpr/all_to_all | solution.py:227
  849.4 16.1 %all-to-all-start = ((bf16[32,2,256]{2,1,0:T(2,128)(2,1)}), bf16[32,2,256]{2,1,0:T(2,128)(2,1)S(1)}, u32[]{:S(2)}, u32[]{:S(2)}) async-start(bf16[32,2,256]{2,1,0:T(2,128)(2,1)} %reshape.2423), calls=%async_computation | async-start | bytes 65536 | tf_op jit(solution)/shard_map/while/body/eval_jaxpr/all_to_all | solution.py:216
  865.5 17.0 %all-to-all-start.1 = ((bf16[32,2,256]{2,1,0:T(2,128)(2,1)}), bf16[32,2,256]{2,1,0:T(2,128)(2,1)S(1)}, u32[]{:S(2)}, u32[]{:S(2)}) async-start(bf16[32,2,256]{2,1,0:T(2,128)(2,1)} %reshape.2427), calls=%async_computation.1 | async-start | bytes 65536 | tf_op jit(solution)/shard_map/while/body/eval_jaxpr/all_to_all | solution.py:215
  898.3 13.8 %all-to-all-start.3 = ((bf16[32,2,256]{2,1,0:T(2,128)(2,1)}), bf16[32,2,256]{2,1,0:T(2,128)(2,1)S(1)}, u32[]{:S(2)}, u32[]{:S(2)}) async-start(bf16[32,2,256]{2,1,0:T(2,128)(2,1)} %reshape.2437), calls=%async_computation.3 | async-start | bytes 65536 | tf_op jit(solution)/shard_map/while/body/eval_jaxpr/all_to_all | solution.py:228
  912.2 13.7 %all-to-all-start.2 = ((bf16[32,2,256]{2,1,0:T(2,128)(2,1)}), bf16[32,2,256]{2,1,0:T(2,128)(2,1)S(1)}, u32[]{:S(2)}, u32[]{:S(2)}) async-start(bf16[32,2,256]{2,1,0:T(2,128)(2,1)} %reshape.2429), calls=%async_computation.2 | async-start | bytes 65536 | tf_op jit(solution)/shard_map/while/body/eval_jaxpr/all_to_all | solution.py:227
  934.2 8.5 collective-permute-start.3
  954.1 16.1 %all-to-all-start = ((bf16[32,2,256]{2,1,0:T(2,128)(2,1)}), bf16[32,2,256]{2,1,0:T(2,128)(2,1)S(1)}, u32[]{:S(2)}, u32[]{:S(2)}) async-start(bf16[32,2,256]{2,1,0:T(2,128)(2,1)} %reshape.2423), calls=%async_computation | async-start | bytes 65536 | tf_op jit(solution)/shard_map/while/body/eval_jaxpr/all_to_all | solution.py:216
  970.2 17.0 %all-to-all-start.1 = ((bf16[32,2,256]{2,1,0:T(2,128)(2,1)}), bf16[32,2,256]{2,1,0:T(2,128)(2,1)S(1)}, u32[]{:S(2)}, u32[]{:S(2)}) async-start(bf16[32,2,256]{2,1,0:T(2,128)(2,1)} %reshape.2427), calls=%async_computation.1 | async-start | bytes 65536 | tf_op jit(solution)/shard_map/while/body/eval_jaxpr/all_to_all | solution.py:215
  1003.0 13.8 %all-to-all-start.3 = ((bf16[32,2,256]{2,1,0:T(2,128)(2,1)}), bf16[32,2,256]{2,1,0:T(2,128)(2,1)S(1)}, u32[]{:S(2)}, u32[]{:S(2)}) async-start(bf16[32,2,256]{2,1,0:T(2,128)(2,1)} %reshape.2437), calls=%async_computation.3 | async-start | bytes 65536 | tf_op jit(solution)/shard_map/while/body/eval_jaxpr/all_to_all | solution.py:228
  1016.9 13.7 %all-to-all-start.2 = ((bf16[32,2,256]{2,1,0:T(2,128)(2,1)}), bf16[32,2,256]{2,1,0:T(2,128)(2,1)S(1)}, u32[]{:S(2)}, u32[]{:S(2)}) async-start(bf16[32,2,256]{2,1,0:T(2,128)(2,1)} %reshape.2429), calls=%async_computation.2 | async-start | bytes 65536 | tf_op jit(solution)/shard_map/while/body/eval_jaxpr/all_to_all | solution.py:227
  (57 other events, 254.2 us)
where the time goes:
time: 1060 us; the launch traced here: 1050 us
  starting transfers between devices  335 us (32%)
  waiting for transfers between devices  264 us (25%)
  matrix products  238 us (22%)
  local copies, waits for them, and re-layouts  129 us (12%)
  other arithmetic  50.5 us (5%)
  loops' own time  35.7 us (3%)
    all_to_all x10, starting transfers between devices, one_tick(): lax.all_to_all(joined_bf16(spec_f), 'rows', split_axis=3, concat_axis=3,...  83.2 us
    all_to_all x10, starting transfers between devices, one_tick(): lax.all_to_all(joined_bf16(spec_a), 'rows', split_axis=3, concat_axis=3,...  77.7 us
    all_to_all x10, waiting for transfers between devices, one_tick(): lax.all_to_all(outgoing[1], 'rows', split_axis=3, concat_axis=3, tiled=True)  72 us
    all_to_all x10, waiting for transfers between devices, one_tick(): lax.all_to_all(joined_bf16(spec_f), 'rows', split_axis=3, concat_axis=3,...  65.2 us
    ppermute x20, starting transfers between devices, extended_2(): after = lax.ppermute(initial, axis, down)  63.4 us
    dot_general x120, matrix products, contract(): product(values[1], matrix[0])  60.7 us
    all_to_all x10, waiting for transfers between devices, one_tick(): lax.all_to_all(outgoing[0], 'rows', split_axis=3, concat_axis=3, tiled=True)  60.3 us
    dot_general x120, matrix products, contract(): product(values[1], matrix[1])  51 us
  transfers between devices with their start and end apart: 100, of which 70 were waited for; matrix products, arithmetic and copies ran while one was open for 12% of the time, Pallas kernels for 0%

commit v1 on v0

v1 whole, which is shorter than its diff:
```python
import math

import jax
import jax.numpy as jnp
from jax import lax
from jax.experimental import pallas as pl
from jax.experimental.pallas import tpu as pltpu
from jax.sharding import PartitionSpec as P

MESH = pl.DeviceIdType.MESH
f32, bf16 = jnp.float32, jnp.bfloat16
HALF = 256
ROWS = 16
NROW = 32
NZ = 8
REF_ROW = 5
CHAINS = ((1, 0), (2, 9), (4, 18), (6, 27))


def chain_depth(c):
    return jnp.where(c == 0, 1, 2 * c)


def chain_row(c):
    return 9 * c


def is_chain_device(d, r):
    hit = jnp.logical_and(d == CHAINS[0][0], r == CHAINS[0][1])
    for cd, cr in CHAINS[1:]:
        hit = jnp.logical_or(hit, jnp.logical_and(d == cd, r == cr))
    return hit


def dot(a, b, precision=None):
    return jnp.dot(a, b, preferred_element_type=f32, precision=precision)


def iota2(shape, dim):
    return lax.broadcasted_iota(jnp.int32, shape, dim)


def exchange(size, flipped=True):
    row, col = iota2((size, size), 0), iota2((size, size), 1)
    target = jnp.where(flipped, size - 1 - row, row)
    return jnp.where(col == target, 1.0, 0.0).astype(f32)


def series(t, coefs):
    total = jnp.full_like(t, coefs[-1])
    for coef in coefs[-2::-1]:
        total = total * t + coef
    return total


COS_LENS = [(-1.0) ** k / math.factorial(2 * k) for k in range(5)]
SIN_LENS = [(-1.0) ** k / math.factorial(2 * k + 1) for k in range(5)]
COS_PHASE = [(-1.0) ** k / math.factorial(2 * k) for k in range(9)]
SIN_PHASE = [(-1.0) ** k / math.factorial(2 * k + 1) for k in range(8)]


def row_slot(r):
    side = r // 16
    block = jnp.where(side == 1, 31 - r, r)
    return side, pl.ds(pl.multiple_of(block * ROWS, ROWS), ROWS)


def kernel(
    slow_ref, corr_ref, src_ref, adj_ref, ref_ref, omega_ref, out_ref,
    prep, prep_plane, prep_slow,
    coef, plane, refs, arrived,
    phase, base, base_t, table, table_t, ridge,
    shipped, xb, gb, eb, wb,
    prep_sem, prep_plane_sem, prep_slow_sem,
    coef_sem, plane_sem, refs_sem, arrived_sem, ship_sem, ask_sem,
):
    d = lax.axis_index("depth")
    r = lax.axis_index("rows")
    side = r // 16
    barrier = pltpu.get_barrier_semaphore()
    chain_here = is_chain_device(d, r)
    me_c = jnp.where(d == 1, 0, d // 2)

    @pl.when(chain_here)
    def _():
        first = jnp.where(me_c < 2, 0, NZ - 1)

        @pl.loop(0, NROW)
        def _(i):
            pl.semaphore_signal(barrier, inc=1, device_id=(first, i), device_id_type=MESH)

        @pl.loop(0, NZ)
        def _(i):
            @pl.when(i != first)
            def _():
                pl.semaphore_signal(barrier, inc=1, device_id=(i, REF_ROW), device_id_type=MESH)

    for c, (cd, cr) in enumerate(CHAINS):
        @pl.when(jnp.logical_or(d != cd, r != cr))
        def _():
            pl.semaphore_signal(barrier, inc=1, device_id=(cd, cr), device_id_type=MESH)

    turn = exchange(ROWS, side == 1)
    flip = exchange(HALF).astype(bf16)
    turn_b = turn.astype(bf16)

    def halves(values):
        turned = dot(turn_b, values).astype(bf16)
        return turned[:, :HALF], dot(turned[:, HALF:], flip).astype(bf16)

    slow_value = ref_ref[0]
    for k, values in enumerate((slow_ref[0] - slow_value, corr_ref[0])):
        left, right = halves(values.astype(bf16))
        prep[k, 0] = left
        prep[k, 1] = right
    prep_slow[...] = jnp.full((8, 128), slow_value, f32)

    def send_prep(c):
        slot_side, slot_rows = row_slot(r)
        return pltpu.make_async_remote_copy(
            prep, coef.at[d, :, :, slot_side, slot_rows, :], prep_sem.at[c], coef_sem.at[d],
            device_id=(chain_depth(c), chain_row(c)), device_id_type=MESH,
        )

    def send_plane(c):
        slot_side, slot_rows = row_slot(r)
        return pltpu.make_async_remote_copy(
            prep_plane.at[c % 2], plane.at[:, :, slot_side, slot_rows, :], prep_plane_sem.at[c % 2], plane_sem,
            device_id=(chain_depth(c), chain_row(c)), device_id_type=MESH,
        )

    def send_slow(c):
        return pltpu.make_async_remote_copy(
            prep_slow, refs.at[d], prep_slow_sem.at[c], refs_sem,
            device_id=(chain_depth(c), chain_row(c)), device_id_type=MESH,
        )

    at_end = jnp.logical_or(d == 0, d == NZ - 1)
    first_chain = jnp.where(d == 0, 0, 2)

    def asked_by(c):
        return jnp.logical_and(d != 0, jnp.logical_or(d != NZ - 1, c < 2))

    @pl.when(d == 0)
    def _():
        for w in range(2):
            for k in range(2):
                left, right = halves(src_ref[w, k])
                prep_plane[w, k, 0] = left
                prep_plane[w, k, 1] = right

    @pl.when(d == NZ - 1)
    def _():
        for w in range(2):
            for k in range(2):
                left, right = halves(adj_ref[w, k])
                prep_plane[w, k, 0] = left
                prep_plane[w, k, 1] = right

    @pl.when(r == REF_ROW)
    def _():
        pl.semaphore_wait(barrier, 4)

        @pl.loop(0, 4)
        def _(c):
            send_slow(c).start()

    @pl.when(jnp.logical_and(at_end, r != REF_ROW))
    def _():
        pl.semaphore_wait(barrier, 2)

    @pl.when(at_end)
    def _():
        for w in range(2):
            send_plane(first_chain + w).start()
        for w in range(2):
            send_prep(first_chain + w).start()

    @pl.when(jnp.logical_not(chain_here))
    def _():
        start = jnp.where(d >= NZ // 2, 2, 0)

        @pl.loop(0, 4)
        def _(i):
            c = lax.rem(i + start, 4)

            @pl.when(asked_by(c))
            def _():
                pl.semaphore_wait(ask_sem.at[c], 1)
                send_prep(c).start()

    def run_chain(source):
        w = me_c % 2
        omega = omega_ref[w]

        def depth_of(step):
            return step if source else NZ - 1 - step

        def ask(depth):
            @pl.loop(0, NROW)
            def _(i):
                @pl.when(jnp.logical_not(is_chain_device(depth, i)))
                def _():
                    pl.semaphore_signal(ask_sem.at[me_c], inc=1, device_id=(depth, i), device_id_type=MESH)

        for p in range(2):
            for dest, dims in ((base, (0, 1)), (base_t, (1, 0))):
                n = iota2((HALF, HALF), dims[0])
                k = iota2((HALF, HALF), dims[1])
                if p == 1:
                    k = jnp.where(k == 0, HALF, k)
                angle = ((2 * n + 1) * k % (4 * HALF)).astype(f32) * (2.0 * math.pi / (4 * HALF))
                dest[p] = (jnp.cos(angle) if p == 0 else jnp.sin(angle)) * 0.0625
            row, col = iota2((HALF, HALF), 0), iota2((HALF, HALF), 1)
            near = jnp.where(jnp.abs(row - col) == 1, 1.0, jnp.where(row == col, -2.0, 0.0))
            corner = jnp.logical_and(row == col, jnp.logical_or(row == 0, row == HALF - 1))
            ridge[p] = jnp.where(corner, -1.0 if p == 0 else -3.0, near).astype(bf16)

        pl.semaphore_wait(barrier, 255)
        for c in range(4):
            @pl.when(c != me_c)
            def _():
                send_prep(c).start()
        slot_side, slot_rows = row_slot(r)
        own = pltpu.make_async_copy(prep, coef.at[d, :, :, slot_side, slot_rows, :], coef_sem.at[d])
        own.start()
        ask(depth_of(1))

        pltpu.make_async_copy(refs, refs, refs_sem).wait()

        unit = 2.0 * math.pi / (2 * HALF)

        def scale_power(depth):
            return (14 * depth) % 16, (14 * depth + 7) % 16

        @pl.loop(0, NZ)
        def _(depth):
            speed = refs[depth, 0:1, 0:1] * omega
            speed2 = speed * speed
            forward_power, inverse_power = scale_power(depth)
            power = (forward_power + inverse_power).astype(f32)
            gain = jnp.exp2(jnp.full((1, 1), 1.0, f32) * power * (-0.125))

            def phase_tile(row, col, row_odd, col_odd):
                gains = gain * jnp.where(row == 0, 0.5, 1.0) * jnp.where(col == 0, 0.5, 1.0)
                row = jnp.where(row == 0, HALF, row) if row_odd else row
                col = jnp.where(col == 0, HALF, col) if col_odd else col
                wave_x, wave_y = row.astype(f32) * unit, col.astype(f32) * unit
                squared = speed2 - wave_x * wave_x - wave_y * wave_y
                damping = jnp.exp(-jnp.sqrt(jnp.maximum(-squared, 0.0))) * gains
                inside = jnp.maximum(squared, 0.0)
                angle = jnp.sqrt(inside)
                return damping * series(inside, COS_PHASE), damping * (series(inside, SIN_PHASE) * angle)

            @pl.loop(0, HALF // 8)
            def _(i):
                rows = pl.ds(pl.multiple_of(i * 8, 8), 8)
                row = iota2((8, HALF), 0) + i * 8
                col = iota2((8, HALF), 1)
                even = phase_tile(row, col, False, False)
                odd = phase_tile(row[:, :128], col[:, :128], False, True)
                for k in range(2):
                    for p in range(2):
                        phase[depth, 0, p, k, rows, :] = even[k]
                        phase[depth, 1, p, k, rows, 0:128] = odd[k]
                        phase[depth, 1, p, k, rows, 128:256] = even[k][:, 128:]

            row, col = iota2((8, HALF), 0), iota2((8, HALF), 1)
            for q in range(2):
                tile = phase_tile(row, col, True, q == 1)
                for k in range(2):
                    phase[depth, q, 1, k, 0:8, :] = tile[k]

        def make_tables(depth):
            forward_power, inverse_power = scale_power(depth)
            for way, power in enumerate((forward_power, inverse_power)):
                scale = jnp.exp2(jnp.full((1, 1), 1.0, f32) * power.astype(f32) * 0.0625)
                for p in range(2):
                    table[way, p] = (base[p] * scale).astype(bf16)
                    table_t[way, p] = (base_t[p] * scale).astype(bf16)

        def propagate(depth):
            for q in range(2):
                for p in range(2):
                    half = dot(xb[q, p].reshape(2 * HALF, HALF), table[0, q]).astype(bf16)
                    real = dot(table_t[0, p], half[:HALF])
                    imag = dot(table_t[0, p], half[HALF:])
                    cos = phase[depth, q, p, 0]
                    sin = phase[depth, q, p, 1]
                    if source:
                        turned = (real * cos - imag * sin, real * sin + imag * cos)
                    else:
                        turned = (real * cos + imag * sin, imag * cos - real * sin)
                    back = [dot(table[1, p], part.astype(bf16)).astype(bf16) for part in turned]
                    for k in range(2):
                        eb[q, p, k] = dot(back[k], table_t[1, q])

        def laplace(blocks, q, p, k):
            values = blocks[q, p, k]
            return dot(values, ridge[q]) + dot(ridge[p], values)

        def unfold(parts):
            mixed = [[parts[q][0] + parts[q][1], parts[q][0] - parts[q][1]] for q in range(2)]
            return [[mixed[0][a] + mixed[1][a] for a in range(2)], [mixed[0][a] - mixed[1][a] for a in range(2)]]

        def tiles(body):
            @pl.loop(0, HALF // ROWS)
            def _(i):
                rows = pl.ds(pl.multiple_of(i * ROWS, ROWS), ROWS)
                for j in range(2):
                    body(rows, pl.ds(j * 128, 128))

        def lens_of(depth, b, a, rows, cols):
            angle = coef[depth, 0, b, a, rows, cols].astype(f32) * omega
            square = angle * angle
            return series(square, COS_LENS), series(square, SIN_LENS) * angle

        def ship(step, depth):
            @pl.loop(0, NROW)
            def _(i):
                to_side, to_rows = row_slot(i)
                block = shipped.at[step, :, :, to_side, to_rows, :]
                here = jnp.logical_and(depth == d, i == r)

                @pl.when(here)
                def _():
                    pltpu.make_async_copy(block, arrived.at[me_c], ship_sem.at[step]).start()

                @pl.when(jnp.logical_not(here))
                def _():
                    pltpu.make_async_remote_copy(
                        block, arrived.at[me_c], ship_sem.at[step], arrived_sem.at[me_c],
                        device_id=(depth, i), device_id_type=MESH,
                    ).start()

        def ask_ahead(step):
            @pl.when(step + 2 < steps)
            def _():
                ask(depth_of(step + 2))

        def wait_coef(depth):
            pltpu.make_async_copy(coef.at[depth], coef.at[depth], coef_sem.at[depth]).wait()

        steps = NZ if source else NZ - 1
        pltpu.make_async_copy(plane, plane, plane_sem).wait()

        def first_fold(rows, cols):
            for k in range(2):
                folded = unfold([[plane[k, b, a, rows, cols].astype(f32) for a in range(2)] for b in range(2)])
                for q in range(2):
                    for p in range(2):
                        if source:
                            xb[q, p, k, rows, cols] = folded[q][p].astype(bf16)
                        else:
                            eb[q, p, k, rows, cols] = folded[q][p] * 0.25
                            gb[q, p, k, rows, cols] = (folded[q][p] * 0.25).astype(bf16)

        tiles(first_fold)

        if source:
            @pl.loop(0, steps)
            def _(step):
                depth = depth_of(step)
                make_tables(depth)
                ask_ahead(step)
                propagate(depth)
                wait_coef(depth)

                def spatial(rows, cols):
                    real = unfold([[eb[q, p, 0, rows, cols] for p in range(2)] for q in range(2)])
                    imag = unfold([[eb[q, p, 1, rows, cols] for p in range(2)] for q in range(2)])
                    lensed = [[[None, None], [None, None]] for _ in range(2)]
                    scaled = [[[None, None], [None, None]] for _ in range(2)]
                    for b in range(2):
                        for a in range(2):
                            cos, sin = lens_of(depth, b, a, rows, cols)
                            factor = coef[depth, 1, b, a, rows, cols].astype(f32)
                            lensed[0][b][a] = real[b][a] * cos - imag[b][a] * sin
                            lensed[1][b][a] = real[b][a] * sin + imag[b][a] * cos
                            for k in range(2):
                                scaled[k][b][a] = lensed[k][b][a] * factor
                    for k in range(2):
                        wave, bend = unfold(lensed[k]), unfold(scaled[k])
                        for q in range(2):
                            for p in range(2):
                                wb[q, p, k, rows, cols] = wave[q][p]
                                gb[q, p, k, rows, cols] = bend[q][p].astype(bf16)

                tiles(spatial)
                for q in range(2):
                    new = []
                    for p in range(2):
                        real = wb[q, p, 0] - laplace(gb, q, p, 1)
                        imag = wb[q, p, 1] + laplace(gb, q, p, 0)
                        xb[q, p, 0] = real.astype(bf16)
                        xb[q, p, 1] = imag.astype(bf16)
                        new.append((real * 0.25, imag * 0.25))
                    for k in range(2):
                        shipped[step, q, k, 0] = (new[0][k] + new[1][k]).astype(bf16)
                        shipped[step, q, k, 1] = (new[0][k] - new[1][k]).astype(bf16)
                ship(step, depth)
        else:
            @pl.loop(0, steps)
            def _(step):
                depth = depth_of(step)
                make_tables(depth)
                ask_ahead(step)
                for q in range(2):
                    for p in range(2):
                        for k in range(2):
                            wb[q, p, k] = laplace(gb, q, p, k)
                wait_coef(depth)

                def spatial(rows, cols):
                    value = [unfold([[eb[q, p, k, rows, cols] for p in range(2)] for q in range(2)]) for k in range(2)]
                    bend = [unfold([[wb[q, p, k, rows, cols] for p in range(2)] for q in range(2)]) for k in range(2)]
                    pulled = [[[None, None], [None, None]] for _ in range(2)]
                    for b in range(2):
                        for a in range(2):
                            cos, sin = lens_of(depth, b, a, rows, cols)
                            factor = coef[depth, 1, b, a, rows, cols].astype(f32)
                            real = value[0][b][a] + factor * bend[1][b][a]
                            imag = value[1][b][a] - factor * bend[0][b][a]
                            pulled[0][b][a] = real * cos + imag * sin
                            pulled[1][b][a] = imag * cos - real * sin
                    for k in range(2):
                        folded = unfold(pulled[k])
                        for q in range(2):
                            for p in range(2):
                                xb[q, p, k, rows, cols] = folded[q][p].astype(bf16)

                tiles(spatial)
                propagate(depth)

                def finish(rows, cols):
                    for q in range(2):
                        for k in range(2):
                            even, odd = eb[q, 0, k, rows, cols], eb[q, 1, k, rows, cols]
                            gb[q, 0, k, rows, cols] = even.astype(bf16)
                            gb[q, 1, k, rows, cols] = odd.astype(bf16)
                            shipped[step, q, k, 0, rows, cols] = (even + odd).astype(bf16)
                            shipped[step, q, k, 1, rows, cols] = (even - odd).astype(bf16)

                tiles(finish)
                ship(step, depth - 1)

        @pl.loop(0, steps)
        def _(step):
            pltpu.make_async_copy(shipped.at[step], shipped.at[step], ship_sem.at[step]).wait()

    @pl.when(jnp.logical_and(chain_here, me_c < 2))
    def _():
        run_chain(True)

    @pl.when(jnp.logical_and(chain_here, me_c >= 2))
    def _():
        run_chain(False)

    def arrival(c):
        @pl.when(jnp.logical_not(jnp.logical_and(chain_here, me_c == c)))
        def _():
            pltpu.make_async_copy(arrived.at[c], arrived.at[c], arrived_sem.at[c]).wait()

    for c in range(2):
        arrival(c)

    @pl.when(d != NZ - 1)
    def _():
        for c in range(2, 4):
            arrival(c)

    last = d == NZ - 1
    total = [None, None]
    for w in range(2):
        below = [[arrived[w, q, k].astype(f32) for k in range(2)] for q in range(2)]
        above = [[arrived[2 + w, q, k].astype(f32) for k in range(2)] for q in range(2)]
        for b in range(2):
            sign = 1.0 if b == 0 else -1.0
            down = [below[0][k] + sign * below[1][k] for k in range(2)]
            up = [
                jnp.where(last, prep_plane[w, k, b].astype(f32), above[0][k] + sign * above[1][k])
                for k in range(2)
            ]
            term = omega_ref[w] * (down[0] * up[1] - down[1] * up[0])
            total[b] = term if total[b] is None else total[b] + term
    exact = lax.Precision.HIGHEST
    total = [dot(turn, part, exact) for part in total]
    out_ref[:, :HALF] = total[0]
    out_ref[:, HALF:] = dot(total[1], exchange(HALF), exact)

    @pl.loop(0, 4)
    def _(c):
        @pl.when(jnp.logical_and(jnp.logical_not(jnp.logical_and(chain_here, me_c == c)), jnp.logical_or(d != 0, c < 2)))
        def _():
            send_prep(c).wait_send()

        @pl.when(r == REF_ROW)
        def _():
            send_slow(c).wait_send()

    @pl.when(at_end)
    def _():
        for w in range(2):
            send_plane(first_chain + w).wait_send()


def per_device(source_top, adjoint_bottom, slowness, correction, slowness_ref, omega):
    vmem = pl.BlockSpec(memory_space=pltpu.VMEM)
    smem = pl.BlockSpec(memory_space=pltpu.SMEM)
    dma, plain = pltpu.SemaphoreType.DMA, pltpu.SemaphoreType.REGULAR
    block = (HALF, HALF)
    gradient = pl.pallas_call(
        kernel,
        out_shape=jax.ShapeDtypeStruct((ROWS, 2 * HALF), f32),
        in_specs=[vmem, vmem, vmem, vmem, smem, smem],
        out_specs=vmem,
        scratch_shapes=[
            pltpu.VMEM((2, 2, ROWS, HALF), bf16),
            pltpu.VMEM((2, 2, 2, ROWS, HALF), bf16),
            pltpu.VMEM((8, 128), f32),
            pltpu.VMEM((NZ, 2, 2, 2) + block, bf16),
            pltpu.VMEM((2, 2, 2) + block, bf16),
            pltpu.VMEM((NZ, 8, 128), f32),
            pltpu.VMEM((4, 2, 2, ROWS, HALF), bf16),
            pltpu.VMEM((NZ, 2, 2, 2) + block, f32),
            pltpu.VMEM((2,) + block, f32),
            pltpu.VMEM((2,) + block, f32),
            pltpu.VMEM((2, 2) + block, bf16),
            pltpu.VMEM((2, 2) + block, bf16),
            pltpu.VMEM((2,) + block, bf16),
            pltpu.VMEM((NZ, 2, 2, 2) + block, bf16),
            pltpu.VMEM((2, 2, 2) + block, bf16),
            pltpu.VMEM((2, 2, 2) + block, bf16),
            pltpu.VMEM((2, 2, 2) + block, f32),
            pltpu.VMEM((2, 2, 2) + block, f32),
            dma((4,)),
            dma((2,)),
            dma((4,)),
            dma((NZ,)),
            dma(()),
            dma(()),
            dma((4,)),
            dma((NZ,)),
            plain((4,)),
        ],
        compiler_params=pltpu.CompilerParams(
            collective_id=0, has_side_effects=True, vmem_limit_bytes=60 * 1024 * 1024
        ),
        name="imaging",
    )(slowness, correction, source_top, adjoint_bottom, slowness_ref, omega)
    return gradient[None]


def solution(mesh):
    in_specs = (
        P(None, None, "rows", None),
        P(None, None, "rows", None),
        P("depth", "rows", None),
        P("depth", "rows", None),
        P("depth"),
        P(),
    )
    return jax.shard_map(
        per_device, mesh=mesh, in_specs=in_specs, out_specs=P("depth", "rows", None), check_vma=False
    )
```

time: 1060 us -> 104 us (0.10)
  starting transfers between devices: 335 us -> 0 us
  waiting for transfers between devices: 264 us -> 0 us
  matrix products: 238 us -> 0 us
  local copies, waits for them, and re-layouts: 129 us -> 1.38 us
  Pallas kernels: 0 us -> 101 us
  other arithmetic: 50.5 us -> 0 us
  loops' own time: 35.7 us -> 0 us
    all_to_all x40 -> x0, starting transfers between devices: 258 us -> none  [the longest x10 83.2 us: one_tick(): lax.all_to_all(joined_bf16(spec_f), 'rows', split_axis=3, concat_axis=3,...]
    all_to_all x40 -> x0, waiting for transfers between devices: 212 us -> none  [the longest x10 72 us: one_tick(): lax.all_to_all(outgoing[1], 'rows', split_axis=3, concat_axis=3, tiled=True)]
    dot_general x480 -> x0, matrix products: 190 us -> none  [the longest x120 60.7 us: contract(): product(values[1], matrix[0])]
    pallas_call x0 -> x1, Pallas kernels: none -> 101 us  [per_device(): pl.pallas_call(kernel, out_shape=jax.ShapeDtypeStruct((ROWS, 2 * HALF), f...]
    ppermute x60 -> x0, starting transfers between devices: 76.5 us -> none  [the longest x20 63.4 us: extended_2(): after = lax.ppermute(initial, axis, down)]
    ppermute x60 -> x0, waiting for transfers between devices: 51.7 us -> none  [the longest x20 26.6 us: extended_2(): before = lax.ppermute(last, axis, up)]
    while x160 -> x0, matrix products: 48.9 us -> none
    while x120 -> x0, local copies, waits for them, and re-layouts: 43.5 us -> none
  transfers between devices with their start and end apart: 100 -> 0, of which waited for: 70 -> 0; matrix products, arithmetic and copies ran while one was open for 12% -> 0% of each run, Pallas kernels for 0% -> 0%
where the time goes in v1:
time: 104 us; the launch traced here: 103 us
  Pallas kernels  101 us (97%)
  local copies, waits for them, and re-layouts  1.38 us (1%)
    pallas_call x1, Pallas kernels, per_device(): pl.pallas_call(kernel, out_shape=jax.ShapeDtypeStruct((ROWS, 2 * HALF), f...  101 us

profile of v1, /device:TPU:32, one launch (start us, length us, event | category | flops | bytes accessed | tf_op | source)
XLA Modules:
  0.0 103.3 jit_solution(12818620862355728618)
XLA Ops:
  0.7 101.2 %imaging.1 = f32[16,512]{1,0:T(8,128)} custom-call(f32[1,16,512]{2,1,0:T(8,128)} %slow_ref.1, f32[1,16,512]{2,1,0:T(8,128)} %corr_ref.1, bf16[2,2,16,512]{3,2,1,0:T(8,128)(2,1)} %src_ref.1, bf16[2,2,16,512]{3,2,1,0:T(8,128)(2,1)} %adj_ref.1, f32[1]{0:T(128)S(6)} %copy.8.ref_ref, f32[2]{0:T(128)} %omega_ref.1), custom_call_target="tpu_custom_call" | custom-call | tf_op jit(solution)/shard_map/imaging/pallas_call | solution.py:512
  101.9 1.4 %copy.9 = f32[1,16,512]{2,1,0:T(8,128)} copy(f32[1,16,512]{2,1,0:T(8,128)} %bitcast.1) | data formatting | bytes 65536

commit v2 on v1

--- a/solution.py
+++ b/solution.py
@@ -14,22 +14,28 @@
 NROW = 32
 NZ = 8
 REF_ROW = 5
-CHAINS = ((1, 0), (2, 9), (4, 18), (6, 27))
 
 
 def chain_depth(c):
-    return jnp.where(c == 0, 1, 2 * c)
+    return 2 + 2 * (c % 2)
 
 
 def chain_row(c):
     return 9 * c
 
 
-def is_chain_device(d, r):
-    hit = jnp.logical_and(d == CHAINS[0][0], r == CHAINS[0][1])
-    for cd, cr in CHAINS[1:]:
-        hit = jnp.logical_or(hit, jnp.logical_and(d == cd, r == cr))
-    return hit
+def on_chain_chip(d, r):
+    return jnp.logical_and(r % 9 == 0, d // 2 == 1 + (r // 9) % 2)
+
+
+def on_edge(d, r):
+    c = r // 8
+    even = jnp.logical_and((r // 4) % 2 == 0, (r + c) % 2 == 1)
+    return jnp.logical_and(even, d == 3 + 2 * (c % 2))
+
+
+def unasked(d, r):
+    return jnp.logical_or(on_chain_chip(d, r), on_edge(d, r))
 
 
 def dot(a, b, precision=None):
@@ -72,14 +78,26 @@
     phase, base, base_t, table, table_t, ridge,
     shipped, xb, gb, eb, wb,
     prep_sem, prep_plane_sem, prep_slow_sem,
-    coef_sem, plane_sem, refs_sem, arrived_sem, ship_sem, ask_sem,
+    coef_sem, plane_sem, refs_sem, arrived_sem, ship_sem, ask_sem, landed_sem, spread_sem, phase_sem, phase_out_sem,
+    edge_sem, ready_sem, relayed, relayed_plane, relay_sem, relay_plane_sem, onward_sem, onward_plane_sem,
 ):
     d = lax.axis_index("depth")
     r = lax.axis_index("rows")
     side = r // 16
     barrier = pltpu.get_barrier_semaphore()
-    chain_here = is_chain_device(d, r)
-    me_c = jnp.where(d == 1, 0, d // 2)
+    z, y = r // 4, r % 4
+    me_c = z // 2
+    chip_here = on_chain_chip(d, r)
+    chain_here = jnp.logical_and(chip_here, d % 2 == 0)
+    helper_here = jnp.logical_and(chip_here, d % 2 == 1)
+    edge_here = on_edge(d, r)
+    relay_here = d == 3 + 2 * (y % 2)
+    at_end = jnp.logical_or(d == 0, d == NZ - 1)
+    first_chain = jnp.where(d == 0, 0, 2)
+    far_c = (y + 2) % 4
+
+    def greet(depth, row):
+        pl.semaphore_signal(barrier, inc=1, device_id=(depth, row), device_id_type=MESH)
 
     @pl.when(chain_here)
     def _():
@@ -87,18 +105,43 @@
 
         @pl.loop(0, NROW)
         def _(i):
-            pl.semaphore_signal(barrier, inc=1, device_id=(first, i), device_id_type=MESH)
-
+            greet(first, i)
+
+        @pl.loop(0, 8)
+        def _(i):
+            @pl.when(i != z)
+            def _():
+                greet(d + 1, 4 * i + y)
+
+        for c in range(4):
+            @pl.when(c != me_c)
+            def _():
+                greet(chain_depth(c), chain_row(c))
+            for other in (1, 3):
+                greet(chain_depth(c) + 1, 8 * c + (c + other) % 4)
+
+    @pl.when(relay_here)
+    def _():
         @pl.loop(0, NZ)
         def _(i):
-            @pl.when(i != first)
-            def _():
-                pl.semaphore_signal(barrier, inc=1, device_id=(i, REF_ROW), device_id_type=MESH)
-
-    for c, (cd, cr) in enumerate(CHAINS):
-        @pl.when(jnp.logical_or(d != cd, r != cr))
+            greet(i, 4 * z + far_c)
+
+    @pl.when(helper_here)
+    def _():
+        greet(d - 1, r)
+
+        @pl.loop(0, NZ)
+        def _(i):
+            greet(i, REF_ROW)
+
+    @pl.when(edge_here)
+    def _():
+        greet(d - 1, 9 * me_c)
+
+    for c in range(4):
+        @pl.when(jnp.logical_or(d != chain_depth(c) + 1, r != chain_row(c)))
         def _():
-            pl.semaphore_signal(barrier, inc=1, device_id=(cd, cr), device_id_type=MESH)
+            greet(chain_depth(c) + 1, chain_row(c))
 
     turn = exchange(ROWS, side == 1)
     flip = exchange(HALF).astype(bf16)
@@ -132,14 +175,51 @@
     def send_slow(c):
         return pltpu.make_async_remote_copy(
             prep_slow, refs.at[d], prep_slow_sem.at[c], refs_sem,
-            device_id=(chain_depth(c), chain_row(c)), device_id_type=MESH,
+            device_id=(chain_depth(c) + 1, chain_row(c)), device_id_type=MESH,
         )
 
-    at_end = jnp.logical_or(d == 0, d == NZ - 1)
-    first_chain = jnp.where(d == 0, 0, 2)
-
-    def asked_by(c):
-        return jnp.logical_and(d != 0, jnp.logical_or(d != NZ - 1, c < 2))
+    far_device = (3 + 2 * (far_c % 2), 4 * z + far_c)
+    far_wanted = jnp.logical_or(d != 0, far_c < 2)
+    far_plane = jnp.logical_and(at_end, far_c // 2 == first_chain // 2)
+
+    def send_far():
+        return pltpu.make_async_remote_copy(
+            prep, relayed.at[d], prep_sem.at[far_c], relay_sem.at[d], device_id=far_device, device_id_type=MESH
+        )
+
+    def send_far_plane():
+        return pltpu.make_async_remote_copy(
+            prep_plane.at[far_c % 2], relayed_plane, prep_plane_sem.at[far_c % 2], relay_plane_sem,
+            device_id=far_device, device_id_type=MESH,
+        )
+
+    passed_side, passed_rows = row_slot(4 * z + far_c)
+    passed_to = (chain_depth(y), chain_row(y))
+
+    def send_onward(depth):
+        return pltpu.make_async_remote_copy(
+            relayed.at[depth], coef.at[depth, :, :, passed_side, passed_rows, :], onward_sem.at[depth], coef_sem.at[depth],
+            device_id=passed_to, device_id_type=MESH,
+        )
+
+    def send_onward_plane():
+        return pltpu.make_async_remote_copy(
+            relayed_plane, plane.at[:, :, passed_side, passed_rows, :], onward_plane_sem, plane_sem,
+            device_id=passed_to, device_id_type=MESH,
+        )
+
+    def pass_plane():
+        pltpu.make_async_copy(relayed_plane, relayed_plane, relay_plane_sem).wait()
+        send_onward_plane().start()
+
+    def pass_depth(depth):
+        pltpu.make_async_copy(relayed.at[depth], relayed.at[depth], relay_sem.at[depth]).wait()
+        send_onward(depth).start()
+
+    relay_steps = jnp.where(y < 2, NZ, NZ - 1)
+
+    def relay_depth(step):
+        return jnp.where(y < 2, step, NZ - 1 - step)
 
     @pl.when(d == 0)
     def _():
@@ -157,51 +237,203 @@
                 prep_plane[w, k, 0] = left
                 prep_plane[w, k, 1] = right
 
+    greetings = 1 + jnp.where(at_end, 2, 0) + jnp.where(r == REF_ROW, 4, 0)
+    greetings = greetings + jnp.where(jnp.logical_and(relay_here, jnp.logical_not(helper_here)), 1, 0)
+    greetings = greetings + jnp.where(edge_here, 4, 0)
+    greetings = jnp.where(chain_here, 7, jnp.where(helper_here, 256, greetings))
+    pl.semaphore_wait(barrier, greetings)
+
+    @pl.when(far_plane)
+    def _():
+        send_far_plane().start()
+
+    @pl.when(at_end)
+    def _():
+        for w in range(2):
+            @pl.when(first_chain + w != far_c)
+            def _():
+                send_plane(first_chain + w).start()
+
+    @pl.when(far_wanted)
+    def _():
+        send_far().start()
+
+    @pl.when(at_end)
+    def _():
+        for w in range(2):
+            @pl.when(first_chain + w != far_c)
+            def _():
+                send_prep(first_chain + w).start()
+
     @pl.when(r == REF_ROW)
     def _():
-        pl.semaphore_wait(barrier, 4)
-
         @pl.loop(0, 4)
         def _(c):
             send_slow(c).start()
 
-    @pl.when(jnp.logical_and(at_end, r != REF_ROW))
-    def _():
-        pl.semaphore_wait(barrier, 2)
-
-    @pl.when(at_end)
-    def _():
-        for w in range(2):
-            send_plane(first_chain + w).start()
-        for w in range(2):
-            send_prep(first_chain + w).start()
-
-    @pl.when(jnp.logical_not(chain_here))
+    @pl.when(jnp.logical_and(relay_here, jnp.logical_not(helper_here)))
+    def _():
+        pass_plane()
+
+        @pl.loop(0, relay_steps)
+        def _(step):
+            pass_depth(relay_depth(step))
+
+    @pl.when(jnp.logical_or(chip_here, edge_here))
+    def _():
+        @pl.loop(0, 4)
+        def _(c):
+            @pl.when(jnp.logical_and(c != far_c, jnp.logical_not(jnp.logical_and(chain_here, c == me_c))))
+            def _():
+                send_prep(c).start()
+
+    @pl.when(jnp.logical_not(jnp.logical_or(chip_here, edge_here)))
     def _():
         start = jnp.where(d >= NZ // 2, 2, 0)
 
         @pl.loop(0, 4)
         def _(i):
             c = lax.rem(i + start, 4)
-
-            @pl.when(asked_by(c))
+            asked = jnp.logical_and(d != 0, jnp.logical_or(d != NZ - 1, c < 2))
+
+            @pl.when(jnp.logical_and(asked, c != far_c))
             def _():
                 pl.semaphore_wait(ask_sem.at[c], 1)
                 send_prep(c).start()
 
+    def spread(step, row):
+        source = me_c < 2
+        target = jnp.where(source, step, NZ - 2 - step)
+        to_side = row // 16
+        block = jnp.where(to_side == 1, 31 - row, row)
+        block = shipped.at[step, :, :, to_side, block // 4, block % 4]
+        here = jnp.logical_and(target == d, row == r)
+
+        @pl.when(here)
+        def _():
+            pltpu.make_async_copy(block, arrived.at[me_c], spread_sem.at[step]).start()
+
+        @pl.when(jnp.logical_not(here))
+        def _():
+            pltpu.make_async_remote_copy(
+                block, arrived.at[me_c], spread_sem.at[step], arrived_sem.at[me_c],
+                device_id=(target, row), device_id_type=MESH,
+            ).start()
+
+    my_steps = jnp.where(me_c < 2, NZ, NZ - 1)
+
+    @pl.when(edge_here)
+    def _():
+        pl.semaphore_wait(ready_sem, 1)
+
+        @pl.loop(0, my_steps)
+        def _(step):
+            pltpu.make_async_copy(shipped.at[step, 0, 0], shipped.at[step, 0, 0], landed_sem.at[step]).wait()
+
+            @pl.loop(0, 8)
+            def _(i):
+                spread(step, 4 * i + y)
+
+        @pl.loop(0, my_steps)
+        def _(step):
+            pltpu.make_async_copy(shipped.at[step, 0, 0], shipped.at[step, 0, 0], spread_sem.at[step]).wait()
+
+    def scale_power(depth):
+        return (14 * depth) % 16, (14 * depth + 7) % 16
+
+    def run_helper():
+        source = me_c < 2
+        omega = omega_ref[me_c % 2]
+        steps = my_steps
+        depth_of = relay_depth
+
+        def ask(step):
+            depth = depth_of(step)
+
+            @pl.when(step < steps)
+            def _():
+                @pl.loop(0, NROW)
+                def _(i):
+                    @pl.when(jnp.logical_not(jnp.logical_or(unasked(depth, i), i % 4 == far_c)))
+                    def _():
+                        pl.semaphore_signal(ask_sem.at[me_c], inc=1, device_id=(depth, i), device_id_type=MESH)
+
+        for other in (1, 3):
+            pl.semaphore_signal(ready_sem, inc=1, device_id=(d, 8 * me_c + (me_c + other) % 4), device_id_type=MESH)
+        ask(1)
+        ask(2)
+        pass_plane()
+        pltpu.make_async_copy(refs, refs, refs_sem).wait()
+        unit = 2.0 * math.pi / (2 * HALF)
+
+        def send_phase(depth):
+            return pltpu.make_async_remote_copy(
+                phase.at[depth], phase.at[depth], phase_out_sem.at[depth], phase_sem.at[depth],
+                device_id=(d - 1, r), device_id_type=MESH,
+            )
+
+        @pl.loop(0, steps)
+        def _(step):
+            depth = depth_of(step)
+            speed = refs[depth, 0:1, 0:1] * omega
+            speed2 = speed * speed
+            forward_power, inverse_power = scale_power(depth)
+            power = (forward_power + inverse_power).astype(f32)
+            gain = jnp.exp2(jnp.full((1, 1), 1.0, f32) * power * (-0.125))
+
+            def phase_tile(row, col, row_odd, col_odd):
+                gains = gain * jnp.where(row == 0, 0.5, 1.0) * jnp.where(col == 0, 0.5, 1.0)
+                row = jnp.where(row == 0, HALF, row) if row_odd else row
+                col = jnp.where(col == 0, HALF, col) if col_odd else col
+                wave_x, wave_y = row.astype(f32) * unit, col.astype(f32) * unit
+                squared = speed2 - wave_x * wave_x - wave_y * wave_y
+                damping = jnp.exp(-jnp.sqrt(jnp.maximum(-squared, 0.0))) * gains
+                inside = jnp.maximum(squared, 0.0)
+                angle = jnp.sqrt(inside)
+                return damping * series(inside, COS_PHASE), damping * (series(inside, SIN_PHASE) * angle)
+
+            @pl.loop(0, HALF // 8)
+            def _(i):
+                rows = pl.ds(pl.multiple_of(i * 8, 8), 8)
+                row = iota2((8, HALF), 0) + i * 8
+                col = iota2((8, HALF), 1)
+                even = phase_tile(row, col, False, False)
+                odd = phase_tile(row[:, :128], col[:, :128], False, True)
+                for k in range(2):
+                    for p in range(2):
+                        phase[depth, 0, p, k, rows, :] = even[k]
+                        phase[depth, 1, p, k, rows, 0:128] = odd[k]
+                        phase[depth, 1, p, k, rows, 128:256] = even[k][:, 128:]
+
+            row, col = iota2((8, HALF), 0), iota2((8, HALF), 1)
+            for q in range(2):
+                tile = phase_tile(row, col, True, q == 1)
+                for k in range(2):
+                    phase[depth, q, 1, k, 0:8, :] = tile[k]
+
+            send_phase(depth).start()
+            pass_depth(depth)
+
+        @pl.loop(0, steps)
+        def _(step):
+            pltpu.make_async_copy(shipped.at[step], shipped.at[step], landed_sem.at[step]).wait()
+            ask(step + 3)
+
+            @pl.loop(0, 16)
+            def _(i):
+                spread(step, 4 * (i // 2) + (y + 2 * (i % 2)) % 4)
+
+        @pl.loop(0, steps)
+        def _(step):
+            send_phase(depth_of(step)).wait_send()
+            pltpu.make_async_copy(shipped.at[step, 0], shipped.at[step, 0], spread_sem.at[step]).wait()
+
     def run_chain(source):
         w = me_c % 2
         omega = omega_ref[w]
 
         def depth_of(step):
             return step if source else NZ - 1 - step
-
-        def ask(depth):
-            @pl.loop(0, NROW)
-            def _(i):
-                @pl.when(jnp.logical_not(is_chain_device(depth, i)))
-                def _():
-                    pl.semaphore_signal(ask_sem.at[me_c], inc=1, device_id=(depth, i), device_id_type=MESH)
 
         for p in range(2):
             for dest, dims in ((base, (0, 1)), (base_t, (1, 0))):
@@ -216,60 +448,9 @@
             corner = jnp.logical_and(row == col, jnp.logical_or(row == 0, row == HALF - 1))
             ridge[p] = jnp.where(corner, -1.0 if p == 0 else -3.0, near).astype(bf16)
 
-        pl.semaphore_wait(barrier, 255)
-        for c in range(4):
-            @pl.when(c != me_c)
-            def _():
-                send_prep(c).start()
         slot_side, slot_rows = row_slot(r)
         own = pltpu.make_async_copy(prep, coef.at[d, :, :, slot_side, slot_rows, :], coef_sem.at[d])
         own.start()
-        ask(depth_of(1))
-
-        pltpu.make_async_copy(refs, refs, refs_sem).wait()
-
-        unit = 2.0 * math.pi / (2 * HALF)
-
-        def scale_power(depth):
-            return (14 * depth) % 16, (14 * depth + 7) % 16
-
-        @pl.loop(0, NZ)
-        def _(depth):
-            speed = refs[depth, 0:1, 0:1] * omega
-            speed2 = speed * speed
-            forward_power, inverse_power = scale_power(depth)
-            power = (forward_power + inverse_power).astype(f32)
-            gain = jnp.exp2(jnp.full((1, 1), 1.0, f32) * power * (-0.125))
-
-            def phase_tile(row, col, row_odd, col_odd):
-                gains = gain * jnp.where(row == 0, 0.5, 1.0) * jnp.where(col == 0, 0.5, 1.0)
-                row = jnp.where(row == 0, HALF, row) if row_odd else row
-                col = jnp.where(col == 0, HALF, col) if col_odd else col
-                wave_x, wave_y = row.astype(f32) * unit, col.astype(f32) * unit
-                squared = speed2 - wave_x * wave_x - wave_y * wave_y
-                damping = jnp.exp(-jnp.sqrt(jnp.maximum(-squared, 0.0))) * gains
-                inside = jnp.maximum(squared, 0.0)
-                angle = jnp.sqrt(inside)
-                return damping * series(inside, COS_PHASE), damping * (series(inside, SIN_PHASE) * angle)
-
-            @pl.loop(0, HALF // 8)
-            def _(i):
-                rows = pl.ds(pl.multiple_of(i * 8, 8), 8)
-                row = iota2((8, HALF), 0) + i * 8
-                col = iota2((8, HALF), 1)
-                even = phase_tile(row, col, False, False)
-                odd = phase_tile(row[:, :128], col[:, :128], False, True)
-                for k in range(2):
-                    for p in range(2):
-                        phase[depth, 0, p, k, rows, :] = even[k]
-                        phase[depth, 1, p, k, rows, 0:128] = odd[k]
-                        phase[depth, 1, p, k, rows, 128:256] = even[k][:, 128:]
-
-            row, col = iota2((8, HALF), 0), iota2((8, HALF), 1)
-            for q in range(2):
-                tile = phase_tile(row, col, True, q == 1)
-                for k in range(2):
-                    phase[depth, q, 1, k, 0:8, :] = tile[k]
 
         def make_tables(depth):
             forward_power, inverse_power = scale_power(depth)
@@ -280,6 +461,7 @@
                     table_t[way, p] = (base_t[p] * scale).astype(bf16)
 
         def propagate(depth):
+            pltpu.make_async_copy(phase.at[depth], phase.at[depth], phase_sem.at[depth]).wait()
             for q in range(2):
                 for p in range(2):
                     half = dot(xb[q, p].reshape(2 * HALF, HALF), table[0, q]).astype(bf16)
@@ -308,35 +490,29 @@
             def _(i):
                 rows = pl.ds(pl.multiple_of(i * ROWS, ROWS), ROWS)
                 for j in range(2):
-                    body(rows, pl.ds(j * 128, 128))
+                    body(i, rows, pl.ds(j * 128, 128))
 
         def lens_of(depth, b, a, rows, cols):
             angle = coef[depth, 0, b, a, rows, cols].astype(f32) * omega
             square = angle * angle
             return series(square, COS_LENS), series(square, SIN_LENS) * angle
 
-        def ship(step, depth):
-            @pl.loop(0, NROW)
-            def _(i):
-                to_side, to_rows = row_slot(i)
-                block = shipped.at[step, :, :, to_side, to_rows, :]
-                here = jnp.logical_and(depth == d, i == r)
-
-                @pl.when(here)
-                def _():
-                    pltpu.make_async_copy(block, arrived.at[me_c], ship_sem.at[step]).start()
-
-                @pl.when(jnp.logical_not(here))
-                def _():
+        def to_helper(step):
+            return pltpu.make_async_remote_copy(
+                shipped.at[step], shipped.at[step], ship_sem.at[step], landed_sem.at[step],
+                device_id=(d + 1, r), device_id_type=MESH,
+            )
+
+        def ship(step):
+            for other in (1, 3):
+                to_y = (y + other) % 4
+                for a, block_y in ((0, to_y), (1, 3 - to_y)):
+                    part = shipped.at[step, :, :, a, :, block_y]
                     pltpu.make_async_remote_copy(
-                        block, arrived.at[me_c], ship_sem.at[step], arrived_sem.at[me_c],
-                        device_id=(depth, i), device_id_type=MESH,
+                        part, part, edge_sem.at[step], landed_sem.at[step],
+                        device_id=(d + 1, 4 * z + to_y), device_id_type=MESH,
                     ).start()
-
-        def ask_ahead(step):
-            @pl.when(step + 2 < steps)
-            def _():
-                ask(depth_of(step + 2))
+            to_helper(step).start()
 
         def wait_coef(depth):
             pltpu.make_async_copy(coef.at[depth], coef.at[depth], coef_sem.at[depth]).wait()
@@ -344,7 +520,7 @@
         steps = NZ if source else NZ - 1
         pltpu.make_async_copy(plane, plane, plane_sem).wait()
 
-        def first_fold(rows, cols):
+        def first_fold(i, rows, cols):
             for k in range(2):
                 folded = unfold([[plane[k, b, a, rows, cols].astype(f32) for a in range(2)] for b in range(2)])
                 for q in range(2):
@@ -362,11 +538,10 @@
             def _(step):
                 depth = depth_of(step)
                 make_tables(depth)
-                ask_ahead(step)
                 propagate(depth)
                 wait_coef(depth)
 
-                def spatial(rows, cols):
+                def spatial(i, rows, cols):
                     real = unfold([[eb[q, p, 0, rows, cols] for p in range(2)] for q in range(2)])
                     imag = unfold([[eb[q, p, 1, rows, cols] for p in range(2)] for q in range(2)])
                     lensed = [[[None, None], [None, None]] for _ in range(2)]
@@ -396,22 +571,21 @@
                         xb[q, p, 1] = imag.astype(bf16)
                         new.append((real * 0.25, imag * 0.25))
                     for k in range(2):
-                        shipped[step, q, k, 0] = (new[0][k] + new[1][k]).astype(bf16)
-                        shipped[step, q, k, 1] = (new[0][k] - new[1][k]).astype(bf16)
-                ship(step, depth)
+                        shipped[step, q, k, 0] = (new[0][k] + new[1][k]).astype(bf16).reshape(4, 4, ROWS, HALF)
+                        shipped[step, q, k, 1] = (new[0][k] - new[1][k]).astype(bf16).reshape(4, 4, ROWS, HALF)
+                ship(step)
         else:
             @pl.loop(0, steps)
             def _(step):
                 depth = depth_of(step)
                 make_tables(depth)
-                ask_ahead(step)
                 for q in range(2):
                     for p in range(2):
                         for k in range(2):
                             wb[q, p, k] = laplace(gb, q, p, k)
                 wait_coef(depth)
 
-                def spatial(rows, cols):
+                def spatial(i, rows, cols):
                     value = [unfold([[eb[q, p, k, rows, cols] for p in range(2)] for q in range(2)]) for k in range(2)]
                     bend = [unfold([[wb[q, p, k, rows, cols] for p in range(2)] for q in range(2)]) for k in range(2)]
                     pulled = [[[None, None], [None, None]] for _ in range(2)]
@@ -432,21 +606,26 @@
                 tiles(spatial)
                 propagate(depth)
 
-                def finish(rows, cols):
+                def finish(i, rows, cols):
                     for q in range(2):
                         for k in range(2):
                             even, odd = eb[q, 0, k, rows, cols], eb[q, 1, k, rows, cols]
                             gb[q, 0, k, rows, cols] = even.astype(bf16)
                             gb[q, 1, k, rows, cols] = odd.astype(bf16)
-                            shipped[step, q, k, 0, rows, cols] = (even + odd).astype(bf16)
-                            shipped[step, q, k, 1, rows, cols] = (even - odd).astype(bf16)
+                            shipped[step, q, k, 0, i // 4, i % 4, :, cols] = (even + odd).astype(bf16)
+                            shipped[step, q, k, 1, i // 4, i % 4, :, cols] = (even - odd).astype(bf16)
 
                 tiles(finish)
-                ship(step, depth - 1)
+                ship(step)
 
         @pl.loop(0, steps)
         def _(step):
-            pltpu.make_async_copy(shipped.at[step], shipped.at[step], ship_sem.at[step]).wait()
+            to_helper(step).wait_send()
+            pltpu.make_async_copy(shipped.at[step, 0], shipped.at[step, 0], edge_sem.at[step]).wait()
+
+    @pl.when(helper_here)
+    def _():
+        run_helper()
 
     @pl.when(jnp.logical_and(chain_here, me_c < 2))
     def _():
@@ -457,7 +636,9 @@
         run_chain(False)
 
     def arrival(c):
-        @pl.when(jnp.logical_not(jnp.logical_and(chain_here, me_c == c)))
+        kept = jnp.logical_and(jnp.logical_or(helper_here, edge_here), me_c == c)
+
+        @pl.when(jnp.logical_not(kept))
         def _():
             pltpu.make_async_copy(arrived.at[c], arrived.at[c], arrived_sem.at[c]).wait()
 
@@ -490,7 +671,9 @@
 
     @pl.loop(0, 4)
     def _(c):
-        @pl.when(jnp.logical_and(jnp.logical_not(jnp.logical_and(chain_here, me_c == c)), jnp.logical_or(d != 0, c < 2)))
+        sent = jnp.logical_and(jnp.logical_not(jnp.logical_and(chain_here, me_c == c)), jnp.logical_or(d != 0, c < 2))
+
+        @pl.when(sent)
         def _():
             send_prep(c).wait_send()
 
@@ -502,6 +685,14 @@
     def _():
         for w in range(2):
             send_plane(first_chain + w).wait_send()
+
+    @pl.when(relay_here)
+    def _():
+        send_onward_plane().wait_send()
+
+        @pl.loop(0, relay_steps)
+        def _(step):
+            send_onward(relay_depth(step)).wait_send()
 
 
 def per_device(source_top, adjoint_bottom, slowness, correction, slowness_ref, omega):
@@ -528,7 +719,7 @@
             pltpu.VMEM((2, 2) + block, bf16),
             pltpu.VMEM((2, 2) + block, bf16),
             pltpu.VMEM((2,) + block, bf16),
-            pltpu.VMEM((NZ, 2, 2, 2) + block, bf16),
+            pltpu.VMEM((NZ, 2, 2, 2, 4, 4, ROWS, HALF), bf16),
             pltpu.VMEM((2, 2, 2) + block, bf16),
             pltpu.VMEM((2, 2, 2) + block, bf16),
             pltpu.VMEM((2, 2, 2) + block, f32),
@@ -542,6 +733,18 @@
             dma((4,)),
             dma((NZ,)),
             plain((4,)),
+            dma((NZ,)),
+            dma((NZ,)),
+            dma((NZ,)),
+            dma((NZ,)),
+            dma((NZ,)),
+            plain(()),
+            pltpu.VMEM((NZ, 2, 2, ROWS, HALF), bf16),
+            pltpu.VMEM((2, 2, ROWS, HALF), bf16),
+            dma((NZ,)),
+            dma(()),
+            dma((NZ,)),
+            dma(()),
         ],
         compiler_params=pltpu.CompilerParams(
             collective_id=0, has_side_effects=True, vmem_limit_bytes=60 * 1024 * 1024

time: 104 us -> 86.4 us (0.83)
  Pallas kernels: 101 us -> 84.2 us
    pallas_call x1, Pallas kernels: 101 us -> 84.2 us  [per_device(): pl.pallas_call(kernel, out_shape=jax.ShapeDtypeStruct((ROWS, 2 * HALF), f...]
where the time goes in v2:
time: 86.4 us; the launch traced here: 86.2 us
  Pallas kernels  84.2 us (97%)
  local copies, waits for them, and re-layouts  1.38 us (2%)
    pallas_call x1, Pallas kernels, per_device(): pl.pallas_call(kernel, out_shape=jax.ShapeDtypeStruct((ROWS, 2 * HALF), f...  84.2 us

profile of v2, /device:TPU:32, one launch (start us, length us, event | category | flops | bytes accessed | tf_op | source)
XLA Modules:
  0.0 86.2 jit_solution(10064888623351757190)
XLA Ops:
  0.7 84.2 %imaging.1 = f32[16,512]{1,0:T(8,128)} custom-call(f32[1,16,512]{2,1,0:T(8,128)} %slow_ref.1, f32[1,16,512]{2,1,0:T(8,128)} %corr_ref.1, bf16[2,2,16,512]{3,2,1,0:T(8,128)(2,1)} %src_ref.1, bf16[2,2,16,512]{3,2,1,0:T(8,128)(2,1)} %adj_ref.1, f32[1]{0:T(128)S(6)} %copy.8.ref_ref, f32[2]{0:T(128)} %omega_ref.1), custom_call_target="tpu_custom_call" | custom-call | tf_op jit(solution)/shard_map/imaging/pallas_call | solution.py:703
  84.8 1.4 %copy.9 = f32[1,16,512]{2,1,0:T(8,128)} copy(f32[1,16,512]{2,1,0:T(8,128)} %bitcast.1) | data formatting | bytes 65536

commit v3 on v2

--- a/solution.py
+++ b/solution.py
@@ -2,6 +2,7 @@
 
 import jax
 import jax.numpy as jnp
+import numpy as np
 from jax import lax
 from jax.experimental import pallas as pl
 from jax.experimental.pallas import tpu as pltpu
@@ -53,14 +54,22 @@
 
 
 def series(t, coefs):
-    total = jnp.full_like(t, coefs[-1])
-    for coef in coefs[-2::-1]:
+    total = t * coefs[-1] + coefs[-2]
+    for coef in coefs[-3::-1]:
         total = total * t + coef
     return total
 
 
-COS_LENS = [(-1.0) ** k / math.factorial(2 * k) for k in range(5)]
-SIN_LENS = [(-1.0) ** k / math.factorial(2 * k + 1) for k in range(5)]
+LENS_REACH = 0.42
+
+
+def fitted(function, reach):
+    fit = np.polynomial.Chebyshev.interpolate(lambda t: function(np.sqrt(np.maximum(t, 1e-30))), 3, domain=(0.0, reach))
+    return [float(coef) for coef in fit.convert(kind=np.polynomial.Polynomial).coef]
+
+
+COS_LENS = fitted(np.cos, LENS_REACH)
+SIN_LENS = fitted(lambda a: np.sin(a) / a, LENS_REACH)
 COS_PHASE = [(-1.0) ** k / math.factorial(2 * k) for k in range(9)]
 SIN_PHASE = [(-1.0) ** k / math.factorial(2 * k + 1) for k in range(8)]
 
@@ -76,7 +85,7 @@
     prep, prep_plane, prep_slow,
     coef, plane, refs, arrived,
     phase, base, base_t, table, table_t, ridge,
-    shipped, xb, gb, eb, wb,
+    shipped, xb, yb, gb, eb, wb,
     prep_sem, prep_plane_sem, prep_slow_sem,
     coef_sem, plane_sem, refs_sem, arrived_sem, ship_sem, ask_sem, landed_sem, spread_sem, phase_sem, phase_out_sem,
     edge_sem, ready_sem, relayed, relayed_plane, relay_sem, relay_plane_sem, onward_sem, onward_plane_sem,
@@ -322,6 +331,17 @@
 
     my_steps = jnp.where(me_c < 2, NZ, NZ - 1)
 
+    def ask(step):
+        depth = jnp.where(me_c < 2, step, NZ - 1 - step)
+
+        @pl.when(step < my_steps)
+        def _():
+            @pl.loop(0, NROW)
+            def _(i):
+                @pl.when(jnp.logical_not(jnp.logical_or(unasked(depth, i), i % 4 == (me_c + 2) % 4)))
+                def _():
+                    pl.semaphore_signal(ask_sem.at[me_c], inc=1, device_id=(depth, i), device_id_type=MESH)
+
     @pl.when(edge_here)
     def _():
         pl.semaphore_wait(ready_sem, 1)
@@ -329,6 +349,10 @@
         @pl.loop(0, my_steps)
         def _(step):
             pltpu.make_async_copy(shipped.at[step, 0, 0], shipped.at[step, 0, 0], landed_sem.at[step]).wait()
+
+            @pl.when(y == (me_c + 1) % 4)
+            def _():
+                ask(step + 4)
 
             @pl.loop(0, 8)
             def _(i):
@@ -347,23 +371,14 @@
         steps = my_steps
         depth_of = relay_depth
 
-        def ask(step):
-            depth = depth_of(step)
-
-            @pl.when(step < steps)
-            def _():
-                @pl.loop(0, NROW)
-                def _(i):
-                    @pl.when(jnp.logical_not(jnp.logical_or(unasked(depth, i), i % 4 == far_c)))
-                    def _():
-                        pl.semaphore_signal(ask_sem.at[me_c], inc=1, device_id=(depth, i), device_id_type=MESH)
-
         for other in (1, 3):
             pl.semaphore_signal(ready_sem, inc=1, device_id=(d, 8 * me_c + (me_c + other) % 4), device_id_type=MESH)
         ask(1)
         ask(2)
+        ask(3)
         pass_plane()
         pltpu.make_async_copy(refs, refs, refs_sem).wait()
+
         unit = 2.0 * math.pi / (2 * HALF)
 
         def send_phase(depth):
@@ -372,8 +387,14 @@
                 device_id=(d - 1, r), device_id_type=MESH,
             )
 
-        @pl.loop(0, steps)
-        def _(step):
+        def forward_rows(step):
+            pltpu.make_async_copy(shipped.at[step], shipped.at[step], landed_sem.at[step]).wait()
+
+            @pl.loop(0, 16)
+            def _(i):
+                spread(step, 4 * (i // 2) + (y + 2 * (i % 2)) % 4)
+
+        def make_phase(step):
             depth = depth_of(step)
             speed = refs[depth, 0:1, 0:1] * omega
             speed2 = speed * speed
@@ -387,10 +408,12 @@
                 col = jnp.where(col == 0, HALF, col) if col_odd else col
                 wave_x, wave_y = row.astype(f32) * unit, col.astype(f32) * unit
                 squared = speed2 - wave_x * wave_x - wave_y * wave_y
-                damping = jnp.exp(-jnp.sqrt(jnp.maximum(-squared, 0.0))) * gains
-                inside = jnp.maximum(squared, 0.0)
-                angle = jnp.sqrt(inside)
-                return damping * series(inside, COS_PHASE), damping * (series(inside, SIN_PHASE) * angle)
+                root = jnp.sqrt(jnp.abs(squared))
+                waving = squared > 0.0
+                inside = jnp.where(waving, squared, 0.0)
+                damping = jnp.where(waving, 1.0, jnp.exp(-root)) * gains
+                sine = jnp.where(waving, series(inside, SIN_PHASE) * root, 0.0)
+                return damping * series(inside, COS_PHASE), damping * sine
 
             @pl.loop(0, HALF // 8)
             def _(i):
@@ -412,16 +435,22 @@
                     phase[depth, q, 1, k, 0:8, :] = tile[k]
 
             send_phase(depth).start()
-            pass_depth(depth)
-
-        @pl.loop(0, steps)
+
+        @pl.loop(-3, steps)
         def _(step):
-            pltpu.make_async_copy(shipped.at[step], shipped.at[step], landed_sem.at[step]).wait()
-            ask(step + 3)
-
-            @pl.loop(0, 16)
-            def _(i):
-                spread(step, 4 * (i // 2) + (y + 2 * (i % 2)) % 4)
+            @pl.when(step >= 0)
+            def _():
+                forward_rows(step)
+
+            @pl.when(step + 3 < steps)
+            def _():
+                make_phase(step + 3)
+
+            @pl.when(step == -3)
+            def _():
+                @pl.loop(0, steps)
+                def _(later):
+                    pass_depth(depth_of(later))
 
         @pl.loop(0, steps)
         def _(step):
@@ -465,17 +494,26 @@
             for q in range(2):
                 for p in range(2):
                     half = dot(xb[q, p].reshape(2 * HALF, HALF), table[0, q]).astype(bf16)
-                    real = dot(table_t[0, p], half[:HALF])
-                    imag = dot(table_t[0, p], half[HALF:])
+                    yb[q, p] = half.reshape(2, HALF, HALF)
+            for p in range(2):
+                for q in range(2):
+                    real = dot(table_t[0, p], yb[q, p, 0])
+                    imag = dot(table_t[0, p], yb[q, p, 1])
                     cos = phase[depth, q, p, 0]
                     sin = phase[depth, q, p, 1]
                     if source:
                         turned = (real * cos - imag * sin, real * sin + imag * cos)
                     else:
                         turned = (real * cos + imag * sin, imag * cos - real * sin)
-                    back = [dot(table[1, p], part.astype(bf16)).astype(bf16) for part in turned]
                     for k in range(2):
-                        eb[q, p, k] = dot(back[k], table_t[1, q])
+                        yb[q, p, k] = turned[k].astype(bf16)
+            for p in range(2):
+                for q in range(2):
+                    for k in range(2):
+                        xb[q, p, k] = dot(table[1, p], yb[q, p, k]).astype(bf16)
+            for q in range(2):
+                for p in range(2):
+                    eb[q, p] = dot(xb[q, p].reshape(2 * HALF, HALF), table_t[1, q]).reshape(2, HALF, HALF)
 
         def laplace(blocks, q, p, k):
             values = blocks[q, p, k]
@@ -492,10 +530,16 @@
                 for j in range(2):
                     body(i, rows, pl.ds(j * 128, 128))
 
+        powers = [omega]
+        for _ in range(6):
+            powers.append(powers[-1] * omega)
+        cos_lens = [COS_LENS[0]] + [COS_LENS[k] * powers[2 * k - 1] for k in range(1, 4)]
+        sin_lens = [SIN_LENS[k] * powers[2 * k] for k in range(4)]
+
         def lens_of(depth, b, a, rows, cols):
-            angle = coef[depth, 0, b, a, rows, cols].astype(f32) * omega
-            square = angle * angle
-            return series(square, COS_LENS), series(square, SIN_LENS) * angle
+            offset = coef[depth, 0, b, a, rows, cols].astype(f32)
+            square = offset * offset
+            return series(square, cos_lens), series(square, sin_lens) * offset
 
         def to_helper(step):
             return pltpu.make_async_remote_copy(
@@ -720,6 +764,7 @@
             pltpu.VMEM((2, 2) + block, bf16),
             pltpu.VMEM((2,) + block, bf16),
             pltpu.VMEM((NZ, 2, 2, 2, 4, 4, ROWS, HALF), bf16),
+            pltpu.VMEM((2, 2, 2) + block, bf16),
             pltpu.VMEM((2, 2, 2) + block, bf16),
             pltpu.VMEM((2, 2, 2) + block, bf16),
             pltpu.VMEM((2, 2, 2) + block, f32),

time: 86.4 us -> 77.3 us (0.89)
  Pallas kernels: 84.2 us -> 75.1 us
    pallas_call x1, Pallas kernels: 84.2 us -> 75.1 us  [per_device(): pl.pallas_call(kernel, out_shape=jax.ShapeDtypeStruct((ROWS, 2 * HALF), f...]
where the time goes in v3:
time: 77.3 us; the launch traced here: 77.1 us
  Pallas kernels  75.1 us (97%)
  local copies, waits for them, and re-layouts  1.38 us (2%)
    pallas_call x1, Pallas kernels, per_device(): pl.pallas_call(kernel, out_shape=jax.ShapeDtypeStruct((ROWS, 2 * HALF), f...  75.1 us

profile of v3, /device:TPU:32, one launch (start us, length us, event | category | flops | bytes accessed | tf_op | source)
XLA Modules:
  0.0 77.1 jit_solution(9629137540225884027)
XLA Ops:
  0.7 75.1 %imaging.1 = f32[16,512]{1,0:T(8,128)} custom-call(f32[1,16,512]{2,1,0:T(8,128)} %slow_ref.1, f32[1,16,512]{2,1,0:T(8,128)} %corr_ref.1, bf16[2,2,16,512]{3,2,1,0:T(8,128)(2,1)} %src_ref.1, bf16[2,2,16,512]{3,2,1,0:T(8,128)(2,1)} %adj_ref.1, f32[1]{0:T(128)S(6)} %copy.8.ref_ref, f32[2]{0:T(128)} %omega_ref.1), custom_call_target="tpu_custom_call" | custom-call | tf_op jit(solution)/shard_map/imaging/pallas_call | solution.py:747
  75.7 1.4 %copy.9 = f32[1,16,512]{2,1,0:T(8,128)} copy(f32[1,16,512]{2,1,0:T(8,128)} %bitcast.1) | data formatting | bytes 65536

commit v4 on v3

--- a/solution.py
+++ b/solution.py
@@ -15,6 +15,7 @@
 NROW = 32
 NZ = 8
 REF_ROW = 5
+FIRST_ROW = 6
 
 
 def chain_depth(c):
@@ -77,7 +78,7 @@
 def row_slot(r):
     side = r // 16
     block = jnp.where(side == 1, 31 - r, r)
-    return side, pl.ds(pl.multiple_of(block * ROWS, ROWS), ROWS)
+    return side, block
 
 
 def kernel(
@@ -88,7 +89,7 @@
     shipped, xb, yb, gb, eb, wb,
     prep_sem, prep_plane_sem, prep_slow_sem,
     coef_sem, plane_sem, refs_sem, arrived_sem, ship_sem, ask_sem, landed_sem, spread_sem, phase_sem, phase_out_sem,
-    edge_sem, ready_sem, relayed, relayed_plane, relay_sem, relay_plane_sem, onward_sem, onward_plane_sem,
+    first_slow_sem, ready_sem, relayed, relay_sem, onward_sem,
 ):
     d = lax.axis_index("depth")
     r = lax.axis_index("rows")
@@ -100,10 +101,15 @@
     chain_here = jnp.logical_and(chip_here, d % 2 == 0)
     helper_here = jnp.logical_and(chip_here, d % 2 == 1)
     edge_here = on_edge(d, r)
-    relay_here = d == 3 + 2 * (y % 2)
+    relay_here = jnp.logical_and(d == 3 + 2 * (y % 2), z != 2 * y)
     at_end = jnp.logical_or(d == 0, d == NZ - 1)
-    first_chain = jnp.where(d == 0, 0, 2)
+    early = jnp.logical_or(d <= 1, d >= NZ - 2)
+    first_chain = jnp.where(d <= 1, 0, 2)
     far_c = (y + 2) % 4
+    far_here = z != 2 * far_c
+
+    def direct(c):
+        return jnp.logical_or(c != far_c, jnp.logical_not(far_here))
 
     def greet(depth, row):
         pl.semaphore_signal(barrier, inc=1, device_id=(depth, row), device_id_type=MESH)
@@ -111,11 +117,17 @@
     @pl.when(chain_here)
     def _():
         first = jnp.where(me_c < 2, 0, NZ - 1)
+
+        second = jnp.where(me_c < 2, 1, NZ - 2)
 
         @pl.loop(0, NROW)
         def _(i):
             greet(first, i)
 
+        @pl.loop(0, NROW)
+        def _(i):
+            greet(second, i)
+
         @pl.loop(0, 8)
         def _(i):
             @pl.when(i != z)
@@ -129,7 +141,7 @@
             for other in (1, 3):
                 greet(chain_depth(c) + 1, 8 * c + (c + other) % 4)
 
-    @pl.when(relay_here)
+    @pl.when(jnp.logical_or(relay_here, helper_here))
     def _():
         @pl.loop(0, NZ)
         def _(i):
@@ -170,14 +182,14 @@
     def send_prep(c):
         slot_side, slot_rows = row_slot(r)
         return pltpu.make_async_remote_copy(
-            prep, coef.at[d, :, :, slot_side, slot_rows, :], prep_sem.at[c], coef_sem.at[d],
+            prep, coef.at[d, slot_side, slot_rows], prep_sem.at[c], coef_sem.at[d],
             device_id=(chain_depth(c), chain_row(c)), device_id_type=MESH,
         )
 
     def send_plane(c):
         slot_side, slot_rows = row_slot(r)
         return pltpu.make_async_remote_copy(
-            prep_plane.at[c % 2], plane.at[:, :, slot_side, slot_rows, :], prep_plane_sem.at[c % 2], plane_sem,
+            prep_plane.at[c % 2], plane.at[slot_side, slot_rows], prep_plane_sem.at[c % 2], plane_sem,
             device_id=(chain_depth(c), chain_row(c)), device_id_type=MESH,
         )
 
@@ -188,18 +200,17 @@
         )
 
     far_device = (3 + 2 * (far_c % 2), 4 * z + far_c)
-    far_wanted = jnp.logical_or(d != 0, far_c < 2)
-    far_plane = jnp.logical_and(at_end, far_c // 2 == first_chain // 2)
+    far_wanted = jnp.logical_and(far_here, jnp.logical_or(d != 0, far_c < 2))
 
     def send_far():
         return pltpu.make_async_remote_copy(
             prep, relayed.at[d], prep_sem.at[far_c], relay_sem.at[d], device_id=far_device, device_id_type=MESH
         )
 
-    def send_far_plane():
+    def send_first_slow(w):
         return pltpu.make_async_remote_copy(
-            prep_plane.at[far_c % 2], relayed_plane, prep_plane_sem.at[far_c % 2], relay_plane_sem,
-            device_id=far_device, device_id_type=MESH,
+            prep_slow, refs.at[d], first_slow_sem.at[w], refs_sem,
+            device_id=(chain_depth(first_chain + w), chain_row(first_chain + w)), device_id_type=MESH,
         )
 
     passed_side, passed_rows = row_slot(4 * z + far_c)
@@ -207,19 +218,9 @@
 
     def send_onward(depth):
         return pltpu.make_async_remote_copy(
-            relayed.at[depth], coef.at[depth, :, :, passed_side, passed_rows, :], onward_sem.at[depth], coef_sem.at[depth],
+            relayed.at[depth], coef.at[depth, passed_side, passed_rows], onward_sem.at[depth], coef_sem.at[depth],
             device_id=passed_to, device_id_type=MESH,
         )
-
-    def send_onward_plane():
-        return pltpu.make_async_remote_copy(
-            relayed_plane, plane.at[:, :, passed_side, passed_rows, :], onward_plane_sem, plane_sem,
-            device_id=passed_to, device_id_type=MESH,
-        )
-
-    def pass_plane():
-        pltpu.make_async_copy(relayed_plane, relayed_plane, relay_plane_sem).wait()
-        send_onward_plane().start()
 
     def pass_depth(depth):
         pltpu.make_async_copy(relayed.at[depth], relayed.at[depth], relay_sem.at[depth]).wait()
@@ -246,224 +247,56 @@
                 prep_plane[w, k, 0] = left
                 prep_plane[w, k, 1] = right
 
-    greetings = 1 + jnp.where(at_end, 2, 0) + jnp.where(r == REF_ROW, 4, 0)
-    greetings = greetings + jnp.where(jnp.logical_and(relay_here, jnp.logical_not(helper_here)), 1, 0)
+    greetings = 1 + jnp.where(early, 2, 0) + jnp.where(r == REF_ROW, 4, 0)
+    greetings = greetings + jnp.where(relay_here, 1, 0)
     greetings = greetings + jnp.where(edge_here, 4, 0)
     greetings = jnp.where(chain_here, 7, jnp.where(helper_here, 256, greetings))
-    pl.semaphore_wait(barrier, greetings)
-
-    @pl.when(far_plane)
-    def _():
-        send_far_plane().start()
-
-    @pl.when(at_end)
-    def _():
-        for w in range(2):
-            @pl.when(first_chain + w != far_c)
-            def _():
-                send_plane(first_chain + w).start()
-
-    @pl.when(far_wanted)
-    def _():
-        send_far().start()
-
-    @pl.when(at_end)
-    def _():
-        for w in range(2):
-            @pl.when(first_chain + w != far_c)
-            def _():
-                send_prep(first_chain + w).start()
-
-    @pl.when(r == REF_ROW)
-    def _():
-        @pl.loop(0, 4)
-        def _(c):
-            send_slow(c).start()
-
-    @pl.when(jnp.logical_and(relay_here, jnp.logical_not(helper_here)))
-    def _():
-        pass_plane()
-
-        @pl.loop(0, relay_steps)
-        def _(step):
-            pass_depth(relay_depth(step))
-
-    @pl.when(jnp.logical_or(chip_here, edge_here))
-    def _():
-        @pl.loop(0, 4)
-        def _(c):
-            @pl.when(jnp.logical_and(c != far_c, jnp.logical_not(jnp.logical_and(chain_here, c == me_c))))
-            def _():
-                send_prep(c).start()
-
-    @pl.when(jnp.logical_not(jnp.logical_or(chip_here, edge_here)))
-    def _():
-        start = jnp.where(d >= NZ // 2, 2, 0)
-
-        @pl.loop(0, 4)
-        def _(i):
-            c = lax.rem(i + start, 4)
-            asked = jnp.logical_and(d != 0, jnp.logical_or(d != NZ - 1, c < 2))
-
-            @pl.when(jnp.logical_and(asked, c != far_c))
-            def _():
-                pl.semaphore_wait(ask_sem.at[c], 1)
-                send_prep(c).start()
-
-    def spread(step, row):
-        source = me_c < 2
-        target = jnp.where(source, step, NZ - 2 - step)
-        to_side = row // 16
-        block = jnp.where(to_side == 1, 31 - row, row)
-        block = shipped.at[step, :, :, to_side, block // 4, block % 4]
-        here = jnp.logical_and(target == d, row == r)
-
-        @pl.when(here)
-        def _():
-            pltpu.make_async_copy(block, arrived.at[me_c], spread_sem.at[step]).start()
-
-        @pl.when(jnp.logical_not(here))
-        def _():
-            pltpu.make_async_remote_copy(
-                block, arrived.at[me_c], spread_sem.at[step], arrived_sem.at[me_c],
-                device_id=(target, row), device_id_type=MESH,
-            ).start()
-
-    my_steps = jnp.where(me_c < 2, NZ, NZ - 1)
-
-    def ask(step):
-        depth = jnp.where(me_c < 2, step, NZ - 1 - step)
-
-        @pl.when(step < my_steps)
-        def _():
-            @pl.loop(0, NROW)
-            def _(i):
-                @pl.when(jnp.logical_not(jnp.logical_or(unasked(depth, i), i % 4 == (me_c + 2) % 4)))
-                def _():
-                    pl.semaphore_signal(ask_sem.at[me_c], inc=1, device_id=(depth, i), device_id_type=MESH)
-
-    @pl.when(edge_here)
-    def _():
-        pl.semaphore_wait(ready_sem, 1)
-
-        @pl.loop(0, my_steps)
-        def _(step):
-            pltpu.make_async_copy(shipped.at[step, 0, 0], shipped.at[step, 0, 0], landed_sem.at[step]).wait()
-
-            @pl.when(y == (me_c + 1) % 4)
-            def _():
-                ask(step + 4)
-
-            @pl.loop(0, 8)
-            def _(i):
-                spread(step, 4 * i + y)
-
-        @pl.loop(0, my_steps)
-        def _(step):
-            pltpu.make_async_copy(shipped.at[step, 0, 0], shipped.at[step, 0, 0], spread_sem.at[step]).wait()
-
     def scale_power(depth):
         return (14 * depth) % 16, (14 * depth + 7) % 16
 
-    def run_helper():
-        source = me_c < 2
-        omega = omega_ref[me_c % 2]
-        steps = my_steps
-        depth_of = relay_depth
-
-        for other in (1, 3):
-            pl.semaphore_signal(ready_sem, inc=1, device_id=(d, 8 * me_c + (me_c + other) % 4), device_id_type=MESH)
-        ask(1)
-        ask(2)
-        ask(3)
-        pass_plane()
-        pltpu.make_async_copy(refs, refs, refs_sem).wait()
-
-        unit = 2.0 * math.pi / (2 * HALF)
-
-        def send_phase(depth):
-            return pltpu.make_async_remote_copy(
-                phase.at[depth], phase.at[depth], phase_out_sem.at[depth], phase_sem.at[depth],
-                device_id=(d - 1, r), device_id_type=MESH,
-            )
-
-        def forward_rows(step):
-            pltpu.make_async_copy(shipped.at[step], shipped.at[step], landed_sem.at[step]).wait()
-
-            @pl.loop(0, 16)
-            def _(i):
-                spread(step, 4 * (i // 2) + (y + 2 * (i % 2)) % 4)
-
-        def make_phase(step):
-            depth = depth_of(step)
-            speed = refs[depth, 0:1, 0:1] * omega
-            speed2 = speed * speed
-            forward_power, inverse_power = scale_power(depth)
-            power = (forward_power + inverse_power).astype(f32)
-            gain = jnp.exp2(jnp.full((1, 1), 1.0, f32) * power * (-0.125))
-
-            def phase_tile(row, col, row_odd, col_odd):
-                gains = gain * jnp.where(row == 0, 0.5, 1.0) * jnp.where(col == 0, 0.5, 1.0)
-                row = jnp.where(row == 0, HALF, row) if row_odd else row
-                col = jnp.where(col == 0, HALF, col) if col_odd else col
-                wave_x, wave_y = row.astype(f32) * unit, col.astype(f32) * unit
-                squared = speed2 - wave_x * wave_x - wave_y * wave_y
-                root = jnp.sqrt(jnp.abs(squared))
-                waving = squared > 0.0
-                inside = jnp.where(waving, squared, 0.0)
-                damping = jnp.where(waving, 1.0, jnp.exp(-root)) * gains
-                sine = jnp.where(waving, series(inside, SIN_PHASE) * root, 0.0)
-                return damping * series(inside, COS_PHASE), damping * sine
-
-            @pl.loop(0, HALF // 8)
-            def _(i):
-                rows = pl.ds(pl.multiple_of(i * 8, 8), 8)
-                row = iota2((8, HALF), 0) + i * 8
-                col = iota2((8, HALF), 1)
-                even = phase_tile(row, col, False, False)
-                odd = phase_tile(row[:, :128], col[:, :128], False, True)
-                for k in range(2):
-                    for p in range(2):
-                        phase[depth, 0, p, k, rows, :] = even[k]
-                        phase[depth, 1, p, k, rows, 0:128] = odd[k]
-                        phase[depth, 1, p, k, rows, 128:256] = even[k][:, 128:]
-
-            row, col = iota2((8, HALF), 0), iota2((8, HALF), 1)
-            for q in range(2):
-                tile = phase_tile(row, col, True, q == 1)
-                for k in range(2):
-                    phase[depth, q, 1, k, 0:8, :] = tile[k]
-
-            send_phase(depth).start()
-
-        @pl.loop(-3, steps)
-        def _(step):
-            @pl.when(step >= 0)
-            def _():
-                forward_rows(step)
-
-            @pl.when(step + 3 < steps)
-            def _():
-                make_phase(step + 3)
-
-            @pl.when(step == -3)
-            def _():
-                @pl.loop(0, steps)
-                def _(later):
-                    pass_depth(depth_of(later))
-
-        @pl.loop(0, steps)
-        def _(step):
-            send_phase(depth_of(step)).wait_send()
-            pltpu.make_async_copy(shipped.at[step, 0], shipped.at[step, 0], spread_sem.at[step]).wait()
-
-    def run_chain(source):
-        w = me_c % 2
-        omega = omega_ref[w]
-
-        def depth_of(step):
-            return step if source else NZ - 1 - step
-
+    unit = 2.0 * math.pi / (2 * HALF)
+
+    def make_phase(depth, omega):
+        speed = refs[depth, 0:1, 0:1] * omega
+        speed2 = speed * speed
+        forward_power, inverse_power = scale_power(depth)
+        power = jnp.asarray(forward_power + inverse_power).astype(f32)
+        gain = jnp.exp2(jnp.full((1, 1), 1.0, f32) * power * (-0.125))
+
+        def phase_tile(row, col, row_odd, col_odd):
+            gains = gain * jnp.where(row == 0, 0.5, 1.0) * jnp.where(col == 0, 0.5, 1.0)
+            row = jnp.where(row == 0, HALF, row) if row_odd else row
+            col = jnp.where(col == 0, HALF, col) if col_odd else col
+            wave_x, wave_y = row.astype(f32) * unit, col.astype(f32) * unit
+            squared = speed2 - wave_x * wave_x - wave_y * wave_y
+            root = jnp.sqrt(jnp.abs(squared))
+            waving = squared > 0.0
+            inside = jnp.where(waving, squared, 0.0)
+            damping = jnp.where(waving, 1.0, jnp.exp(-root)) * gains
+            sine = jnp.where(waving, series(inside, SIN_PHASE) * root, 0.0)
+            return damping * series(inside, COS_PHASE), damping * sine
+
+        @pl.loop(0, HALF // 8)
+        def _(i):
+            rows = pl.ds(pl.multiple_of(i * 8, 8), 8)
+            row = iota2((8, HALF), 0) + i * 8
+            col = iota2((8, HALF), 1)
+            even = phase_tile(row, col, False, False)
+            odd = phase_tile(row[:, :128], col[:, :128], False, True)
+            for k in range(2):
+                for p in range(2):
+                    phase[depth, 0, p, k, rows, :] = even[k]
+                    phase[depth, 1, p, k, rows, 0:128] = odd[k]
+                    phase[depth, 1, p, k, rows, 128:256] = even[k][:, 128:]
+
+        row, col = iota2((8, HALF), 0), iota2((8, HALF), 1)
+        for q in range(2):
+            tile = phase_tile(row, col, True, q == 1)
+            for k in range(2):
+                phase[depth, q, 1, k, 0:8, :] = tile[k]
+
+    @pl.when(chain_here)
+    def _():
         for p in range(2):
             for dest, dims in ((base, (0, 1)), (base_t, (1, 0))):
                 n = iota2((HALF, HALF), dims[0])
@@ -477,8 +310,189 @@
             corner = jnp.logical_and(row == col, jnp.logical_or(row == 0, row == HALF - 1))
             ridge[p] = jnp.where(corner, -1.0 if p == 0 else -3.0, near).astype(bf16)
 
+        first = jnp.where(me_c < 2, 0, NZ - 1)
+        pltpu.make_async_copy(refs.at[first], refs.at[first], refs_sem).wait()
+        make_phase(first, omega_ref[me_c % 2])
+
+    @pl.when(helper_here)
+    def _():
+        pltpu.make_async_copy(refs, refs, refs_sem).wait()
+
+    pl.semaphore_wait(barrier, greetings)
+
+    @pl.when(jnp.logical_and(at_end, r == FIRST_ROW))
+    def _():
+        for w in range(2):
+            send_first_slow(w).start()
+
+    @pl.when(r == REF_ROW)
+    def _():
+        @pl.loop(0, 4)
+        def _(c):
+            send_slow(c).start()
+
+    @pl.when(at_end)
+    def _():
+        for w in range(2):
+            send_plane(first_chain + w).start()
+        for w in range(2):
+            send_plane(first_chain + w).wait_send()
+
+    @pl.when(far_wanted)
+    def _():
+        send_far().start()
+
+    @pl.when(early)
+    def _():
+        for w in range(2):
+            @pl.when(direct(first_chain + w))
+            def _():
+                send_prep(first_chain + w).start()
+
+    @pl.when(relay_here)
+    def _():
+        @pl.loop(0, relay_steps)
+        def _(step):
+            pass_depth(relay_depth(step))
+
+    @pl.when(jnp.logical_or(chip_here, edge_here))
+    def _():
+        @pl.loop(0, 4)
+        def _(c):
+            @pl.when(jnp.logical_and(direct(c), jnp.logical_not(jnp.logical_and(chain_here, c == me_c))))
+            def _():
+                send_prep(c).start()
+
+    @pl.when(jnp.logical_not(jnp.logical_or(chip_here, edge_here)))
+    def _():
+        start = jnp.where(d >= NZ // 2, 2, 0)
+
+        @pl.loop(0, 4)
+        def _(i):
+            c = lax.rem(i + start, 4)
+            asked = jnp.logical_and(d != 0, jnp.logical_not(jnp.logical_and(early, c // 2 == first_chain // 2)))
+
+            @pl.when(jnp.logical_and(asked, direct(c)))
+            def _():
+                pl.semaphore_wait(ask_sem.at[c], 1)
+                send_prep(c).start()
+
+    def spread(step, row):
+        source = me_c < 2
+        target = jnp.where(source, step, NZ - 2 - step)
+        to_side = row // 16
+        block = jnp.where(to_side == 1, 31 - row, row)
+        block = shipped.at[step, row % 4, to_side, block // 4]
+        here = jnp.logical_and(target == d, row == r)
+
+        @pl.when(here)
+        def _():
+            pltpu.make_async_copy(block, arrived.at[me_c], spread_sem.at[step]).start()
+
+        @pl.when(jnp.logical_not(here))
+        def _():
+            pltpu.make_async_remote_copy(
+                block, arrived.at[me_c], spread_sem.at[step], arrived_sem.at[me_c],
+                device_id=(target, row), device_id_type=MESH,
+            ).start()
+
+    my_steps = jnp.where(me_c < 2, NZ, NZ - 1)
+
+    def ask(step):
+        depth = jnp.where(me_c < 2, step, NZ - 1 - step)
+
+        @pl.when(step < my_steps)
+        def _():
+            @pl.loop(0, NROW)
+            def _(i):
+                @pl.when(jnp.logical_not(jnp.logical_or(unasked(depth, i), jnp.logical_and(i % 4 == (me_c + 2) % 4, i // 4 != 2 * me_c))))
+                def _():
+                    pl.semaphore_signal(ask_sem.at[me_c], inc=1, device_id=(depth, i), device_id_type=MESH)
+
+    @pl.when(edge_here)
+    def _():
+        pl.semaphore_wait(ready_sem, 1)
+
+        @pl.when(y == (me_c + 1) % 4)
+        def _():
+            ask(2)
+            ask(3)
+            ask(4)
+
+        @pl.loop(0, my_steps)
+        def _(step):
+            pltpu.make_async_copy(shipped.at[step, 0], shipped.at[step, 0], landed_sem.at[step]).wait()
+
+            @pl.when(y == (me_c + 1) % 4)
+            def _():
+                ask(step + 5)
+
+            @pl.loop(0, 8)
+            def _(i):
+                spread(step, 4 * i + y)
+
+        @pl.loop(0, my_steps)
+        def _(step):
+            pltpu.make_async_copy(shipped.at[step, 0], shipped.at[step, 0], spread_sem.at[step]).wait()
+
+    def run_helper():
+        source = me_c < 2
+        omega = omega_ref[me_c % 2]
+        steps = my_steps
+        depth_of = relay_depth
+
+        for other in (1, 3):
+            pl.semaphore_signal(ready_sem, inc=1, device_id=(d, 8 * me_c + (me_c + other) % 4), device_id_type=MESH)
+
+        def send_phase(depth):
+            return pltpu.make_async_remote_copy(
+                phase.at[depth], phase.at[depth], phase_out_sem.at[depth], phase_sem.at[depth],
+                device_id=(d - 1, r), device_id_type=MESH,
+            )
+
+        def forward_rows(step):
+            half = shipped.at[step, pl.ds(0, 2)]
+            pltpu.make_async_copy(half, half, landed_sem.at[step]).wait()
+
+            @pl.loop(0, 16)
+            def _(i):
+                spread(step, 4 * (i // 2) + (y + 2 * (i % 2)) % 4)
+
+        make_phase(depth_of(1), omega)
+        send_phase(depth_of(1)).start()
+
+        @pl.loop(-2, steps)
+        def _(step):
+            @pl.when(step >= 0)
+            def _():
+                forward_rows(step)
+
+            @pl.when(step + 4 < steps)
+            def _():
+                depth = depth_of(step + 4)
+                make_phase(depth, omega)
+                send_phase(depth).start()
+
+        @pl.loop(0, steps)
+        def _(step):
+            @pl.when(step > 0)
+            def _():
+                send_phase(depth_of(step)).wait_send()
+
+            half = shipped.at[step, pl.ds(0, 2)]
+            pltpu.make_async_copy(half, half, spread_sem.at[step]).wait()
+
+    def run_chain(source):
+        w = me_c % 2
+        omega = omega_ref[w]
+
+        first_depth = 0 if source else NZ - 1
+
+        def depth_of(step):
+            return step if source else NZ - 1 - step
+
         slot_side, slot_rows = row_slot(r)
-        own = pltpu.make_async_copy(prep, coef.at[d, :, :, slot_side, slot_rows, :], coef_sem.at[d])
+        own = pltpu.make_async_copy(prep, coef.at[d, slot_side, slot_rows], coef_sem.at[d])
         own.start()
 
         def make_tables(depth):
@@ -490,7 +504,10 @@
                     table_t[way, p] = (base_t[p] * scale).astype(bf16)
 
         def propagate(depth):
-            pltpu.make_async_copy(phase.at[depth], phase.at[depth], phase_sem.at[depth]).wait()
+            @pl.when(depth != first_depth)
+            def _():
+                pltpu.make_async_copy(phase.at[depth], phase.at[depth], phase_sem.at[depth]).wait()
+
             for q in range(2):
                 for p in range(2):
                     half = dot(xb[q, p].reshape(2 * HALF, HALF), table[0, q]).astype(bf16)
@@ -536,27 +553,22 @@
         cos_lens = [COS_LENS[0]] + [COS_LENS[k] * powers[2 * k - 1] for k in range(1, 4)]
         sin_lens = [SIN_LENS[k] * powers[2 * k] for k in range(4)]
 
-        def lens_of(depth, b, a, rows, cols):
-            offset = coef[depth, 0, b, a, rows, cols].astype(f32)
+        def lens_of(depth, b, a, i, cols):
+            offset = coef[depth, a, i, 0, b, :, cols].astype(f32)
             square = offset * offset
             return series(square, cos_lens), series(square, sin_lens) * offset
 
-        def to_helper(step):
+        def ship_part(step, other):
+            to_y = (y + other) % 4
+            part = shipped.at[step, to_y]
+            to_row = 4 * z + (to_y if other % 2 else y)
             return pltpu.make_async_remote_copy(
-                shipped.at[step], shipped.at[step], ship_sem.at[step], landed_sem.at[step],
-                device_id=(d + 1, r), device_id_type=MESH,
+                part, part, ship_sem.at[step], landed_sem.at[step], device_id=(d + 1, to_row), device_id_type=MESH
             )
 
         def ship(step):
-            for other in (1, 3):
-                to_y = (y + other) % 4
-                for a, block_y in ((0, to_y), (1, 3 - to_y)):
-                    part = shipped.at[step, :, :, a, :, block_y]
-                    pltpu.make_async_remote_copy(
-                        part, part, edge_sem.at[step], landed_sem.at[step],
-                        device_id=(d + 1, 4 * z + to_y), device_id_type=MESH,
-                    ).start()
-            to_helper(step).start()
+            for other in (1, 3, 0, 2):
+                ship_part(step, other).start()
 
         def wait_coef(depth):
             pltpu.make_async_copy(coef.at[depth], coef.at[depth], coef_sem.at[depth]).wait()
@@ -566,7 +578,7 @@
 
         def first_fold(i, rows, cols):
             for k in range(2):
-                folded = unfold([[plane[k, b, a, rows, cols].astype(f32) for a in range(2)] for b in range(2)])
+                folded = unfold([[plane[a, i, k, b, :, cols].astype(f32) for a in range(2)] for b in range(2)])
                 for q in range(2):
                     for p in range(2):
                         if source:
@@ -592,8 +604,8 @@
                     scaled = [[[None, None], [None, None]] for _ in range(2)]
                     for b in range(2):
                         for a in range(2):
-                            cos, sin = lens_of(depth, b, a, rows, cols)
-                            factor = coef[depth, 1, b, a, rows, cols].astype(f32)
+                            cos, sin = lens_of(depth, b, a, i, cols)
+                            factor = coef[depth, a, i, 1, b, :, cols].astype(f32)
                             lensed[0][b][a] = real[b][a] * cos - imag[b][a] * sin
                             lensed[1][b][a] = real[b][a] * sin + imag[b][a] * cos
                             for k in range(2):
@@ -615,8 +627,11 @@
                         xb[q, p, 1] = imag.astype(bf16)
                         new.append((real * 0.25, imag * 0.25))
                     for k in range(2):
-                        shipped[step, q, k, 0] = (new[0][k] + new[1][k]).astype(bf16).reshape(4, 4, ROWS, HALF)
-                        shipped[step, q, k, 1] = (new[0][k] - new[1][k]).astype(bf16).reshape(4, 4, ROWS, HALF)
+                        sides = ((new[0][k] + new[1][k]).astype(bf16), (new[0][k] - new[1][k]).astype(bf16))
+                        for a, values in enumerate(sides):
+                            values = values.reshape(4, 4, ROWS, HALF)
+                            for i in range(4):
+                                shipped[step, i if a == 0 else 3 - i, a, :, q, k] = values[:, i]
                 ship(step)
         else:
             @pl.loop(0, steps)
@@ -635,8 +650,8 @@
                     pulled = [[[None, None], [None, None]] for _ in range(2)]
                     for b in range(2):
                         for a in range(2):
-                            cos, sin = lens_of(depth, b, a, rows, cols)
-                            factor = coef[depth, 1, b, a, rows, cols].astype(f32)
+                            cos, sin = lens_of(depth, b, a, i, cols)
+                            factor = coef[depth, a, i, 1, b, :, cols].astype(f32)
                             real = value[0][b][a] + factor * bend[1][b][a]
                             imag = value[1][b][a] - factor * bend[0][b][a]
                             pulled[0][b][a] = real * cos + imag * sin
@@ -656,16 +671,15 @@
                             even, odd = eb[q, 0, k, rows, cols], eb[q, 1, k, rows, cols]
                             gb[q, 0, k, rows, cols] = even.astype(bf16)
                             gb[q, 1, k, rows, cols] = odd.astype(bf16)
-                            shipped[step, q, k, 0, i // 4, i % 4, :, cols] = (even + odd).astype(bf16)
-                            shipped[step, q, k, 1, i // 4, i % 4, :, cols] = (even - odd).astype(bf16)
+                            shipped[step, i % 4, 0, i // 4, q, k, :, cols] = (even + odd).astype(bf16)
+                            shipped[step, 3 - i % 4, 1, i // 4, q, k, :, cols] = (even - odd).astype(bf16)
 
                 tiles(finish)
                 ship(step)
 
         @pl.loop(0, steps)
         def _(step):
-            to_helper(step).wait_send()
-            pltpu.make_async_copy(shipped.at[step, 0], shipped.at[step, 0], edge_sem.at[step]).wait()
+            pltpu.make_async_copy(shipped.at[step], shipped.at[step], ship_sem.at[step]).wait()
 
     @pl.when(helper_here)
     def _():
@@ -725,15 +739,13 @@
         def _():
             send_slow(c).wait_send()
 
-    @pl.when(at_end)
+    @pl.when(jnp.logical_and(at_end, r == FIRST_ROW))
     def _():
         for w in range(2):
-            send_plane(first_chain + w).wait_send()
+            send_first_slow(w).wait_send()
 
     @pl.when(relay_here)
     def _():
-        send_onward_plane().wait_send()
-
         @pl.loop(0, relay_steps)
         def _(step):
             send_onward(relay_depth(step)).wait_send()
@@ -753,8 +765,8 @@
             pltpu.VMEM((2, 2, ROWS, HALF), bf16),
             pltpu.VMEM((2, 2, 2, ROWS, HALF), bf16),
             pltpu.VMEM((8, 128), f32),
-            pltpu.VMEM((NZ, 2, 2, 2) + block, bf16),
-            pltpu.VMEM((2, 2, 2) + block, bf16),
+            pltpu.VMEM((NZ, 2, 16, 2, 2, ROWS, HALF), bf16),
+            pltpu.VMEM((2, 16, 2, 2, ROWS, HALF), bf16),
             pltpu.VMEM((NZ, 8, 128), f32),
             pltpu.VMEM((4, 2, 2, ROWS, HALF), bf16),
             pltpu.VMEM((NZ, 2, 2, 2) + block, f32),
@@ -763,7 +775,7 @@
             pltpu.VMEM((2, 2) + block, bf16),
             pltpu.VMEM((2, 2) + block, bf16),
             pltpu.VMEM((2,) + block, bf16),
-            pltpu.VMEM((NZ, 2, 2, 2, 4, 4, ROWS, HALF), bf16),
+            pltpu.VMEM((NZ, 4, 2, 4, 2, 2, ROWS, HALF), bf16),
             pltpu.VMEM((2, 2, 2) + block, bf16),
             pltpu.VMEM((2, 2, 2) + block, bf16),
             pltpu.VMEM((2, 2, 2) + block, bf16),
@@ -782,14 +794,11 @@
             dma((NZ,)),
             dma((NZ,)),
             dma((NZ,)),
-            dma((NZ,)),
+            dma((2,)),
             plain(()),
             pltpu.VMEM((NZ, 2, 2, ROWS, HALF), bf16),
-            pltpu.VMEM((2, 2, ROWS, HALF), bf16),
             dma((NZ,)),
-            dma(()),
             dma((NZ,)),
-            dma(()),
         ],
         compiler_params=pltpu.CompilerParams(
             collective_id=0, has_side_effects=True, vmem_limit_bytes=60 * 1024 * 1024

time: 77.3 us -> 72.9 us (0.943)
  Pallas kernels: 75.1 us -> 69.9 us
    pallas_call x1, Pallas kernels: 75.1 us -> 69.9 us  [per_device(): pl.pallas_call(kernel, out_shape=jax.ShapeDtypeStruct((ROWS, 2 * HALF), f...]
where the time goes in v4:
time: 72.9 us; the launch traced here: 72 us
  Pallas kernels  69.9 us (96%)
  local copies, waits for them, and re-layouts  1.38 us (2%)
    pallas_call x1, Pallas kernels, per_device(): pl.pallas_call(kernel, out_shape=jax.ShapeDtypeStruct((ROWS, 2 * HALF), f...  69.9 us

profile of v4, /device:TPU:32, one launch (start us, length us, event | category | flops | bytes accessed | tf_op | source)
XLA Modules:
  0.0 72.0 jit_solution(10868653257831826247)
XLA Ops:
  0.7 69.9 %imaging.1 = f32[16,512]{1,0:T(8,128)} custom-call(f32[1,16,512]{2,1,0:T(8,128)} %slow_ref.1, f32[1,16,512]{2,1,0:T(8,128)} %corr_ref.1, bf16[2,2,16,512]{3,2,1,0:T(8,128)(2,1)} %src_ref.1, bf16[2,2,16,512]{3,2,1,0:T(8,128)(2,1)} %adj_ref.1, f32[1]{0:T(128)S(6)} %copy.8.ref_ref, f32[2]{0:T(128)} %omega_ref.1), custom_call_target="tpu_custom_call" | custom-call | tf_op jit(solution)/shard_map/imaging/pallas_call | solution.py:759
  70.6 1.4 %copy.9 = f32[1,16,512]{2,1,0:T(8,128)} copy(f32[1,16,512]{2,1,0:T(8,128)} %bitcast.1) | data formatting | bytes 65536

commit v5 on v4

--- a/solution.py
+++ b/solution.py
@@ -503,7 +503,13 @@
                     table[way, p] = (base[p] * scale).astype(bf16)
                     table_t[way, p] = (base_t[p] * scale).astype(bf16)
 
-        def propagate(depth):
+        def pack(step, q, k, even, odd):
+            for a, values in enumerate(((even + odd).astype(bf16), (even - odd).astype(bf16))):
+                values = values.reshape(4, 4, ROWS, HALF)
+                for i in range(4):
+                    shipped[step, i if a == 0 else 3 - i, a, :, q, k] = values[:, i]
+
+        def propagate(depth, step):
             @pl.when(depth != first_depth)
             def _():
                 pltpu.make_async_copy(phase.at[depth], phase.at[depth], phase_sem.at[depth]).wait()
@@ -529,8 +535,16 @@
                     for k in range(2):
                         xb[q, p, k] = dot(table[1, p], yb[q, p, k]).astype(bf16)
             for q in range(2):
+                parts = []
                 for p in range(2):
-                    eb[q, p] = dot(xb[q, p].reshape(2 * HALF, HALF), table_t[1, q]).reshape(2, HALF, HALF)
+                    part = dot(xb[q, p].reshape(2 * HALF, HALF), table_t[1, q]).reshape(2, HALF, HALF)
+                    eb[q, p] = part
+                    parts.append(part)
+                if not source:
+                    for p in range(2):
+                        gb[q, p] = parts[p].astype(bf16)
+                    for k in range(2):
+                        pack(step, q, k, parts[0][k], parts[1][k])
 
         def laplace(blocks, q, p, k):
             values = blocks[q, p, k]
@@ -594,7 +608,7 @@
             def _(step):
                 depth = depth_of(step)
                 make_tables(depth)
-                propagate(depth)
+                propagate(depth, step)
                 wait_coef(depth)
 
                 def spatial(i, rows, cols):
@@ -627,11 +641,7 @@
                         xb[q, p, 1] = imag.astype(bf16)
                         new.append((real * 0.25, imag * 0.25))
                     for k in range(2):
-                        sides = ((new[0][k] + new[1][k]).astype(bf16), (new[0][k] - new[1][k]).astype(bf16))
-                        for a, values in enumerate(sides):
-                            values = values.reshape(4, 4, ROWS, HALF)
-                            for i in range(4):
-                                shipped[step, i if a == 0 else 3 - i, a, :, q, k] = values[:, i]
+                        pack(step, q, k, new[0][k], new[1][k])
                 ship(step)
         else:
             @pl.loop(0, steps)
@@ -663,18 +673,8 @@
                                 xb[q, p, k, rows, cols] = folded[q][p].astype(bf16)
 
                 tiles(spatial)
-                propagate(depth)
-
-                def finish(i, rows, cols):
-                    for q in range(2):
-                        for k in range(2):
-                            even, odd = eb[q, 0, k, rows, cols], eb[q, 1, k, rows, cols]
-                            gb[q, 0, k, rows, cols] = even.astype(bf16)
-                            gb[q, 1, k, rows, cols] = odd.astype(bf16)
-                            shipped[step, i % 4, 0, i // 4, q, k, :, cols] = (even + odd).astype(bf16)
-                            shipped[step, 3 - i % 4, 1, i // 4, q, k, :, cols] = (even - odd).astype(bf16)
-
-                tiles(finish)
+                propagate(depth, step)
+
                 ship(step)
 
         @pl.loop(0, steps)

time: 72.9 us -> 69.9 us (0.959)
  Pallas kernels: 69.9 us -> 67.1 us
    pallas_call x1, Pallas kernels: 69.9 us -> 67.1 us  [per_device(): pl.pallas_call(kernel, out_shape=jax.ShapeDtypeStruct((ROWS, 2 * HALF), f...]
where the time goes in v5:
time: 69.9 us; the launch traced here: 69.2 us
  Pallas kernels  67.1 us (96%)
  local copies, waits for them, and re-layouts  1.38 us (2%)
    pallas_call x1, Pallas kernels, per_device(): pl.pallas_call(kernel, out_shape=jax.ShapeDtypeStruct((ROWS, 2 * HALF), f...  67.1 us

profile of v5, /device:TPU:32, one launch (start us, length us, event | category | flops | bytes accessed | tf_op | source)
XLA Modules:
  0.0 69.2 jit_solution(4593791398668754017)
XLA Ops:
  0.7 67.1 %imaging.1 = f32[16,512]{1,0:T(8,128)} custom-call(f32[1,16,512]{2,1,0:T(8,128)} %slow_ref.1, f32[1,16,512]{2,1,0:T(8,128)} %corr_ref.1, bf16[2,2,16,512]{3,2,1,0:T(8,128)(2,1)} %src_ref.1, bf16[2,2,16,512]{3,2,1,0:T(8,128)(2,1)} %adj_ref.1, f32[1]{0:T(128)S(6)} %copy.8.ref_ref, f32[2]{0:T(128)} %omega_ref.1), custom_call_target="tpu_custom_call" | custom-call | tf_op jit(solution)/shard_map/imaging/pallas_call | solution.py:759
  67.8 1.4 %copy.9 = f32[1,16,512]{2,1,0:T(8,128)} copy(f32[1,16,512]{2,1,0:T(8,128)} %bitcast.1) | data formatting | bytes 65536

commit v6 on v5

--- a/solution.py
+++ b/solution.py
@@ -555,7 +555,7 @@
             return [[mixed[0][a] + mixed[1][a] for a in range(2)], [mixed[0][a] - mixed[1][a] for a in range(2)]]
 
         def tiles(body):
-            @pl.loop(0, HALF // ROWS)
+            @pl.loop(0, HALF // ROWS, unroll=2)
             def _(i):
                 rows = pl.ds(pl.multiple_of(i * ROWS, ROWS), ROWS)
                 for j in range(2):

time: 69.9 us -> 69.3 us (level)
  no operation moved by 1% of the time
where the time goes in v6:
time: 69.3 us; the launch traced here: 69 us
  Pallas kernels  66.9 us (97%)
  local copies, waits for them, and re-layouts  1.38 us (2%)
    pallas_call x1, Pallas kernels, per_device(): pl.pallas_call(kernel, out_shape=jax.ShapeDtypeStruct((ROWS, 2 * HALF), f...  66.9 us

profile of v6, /device:TPU:32, one launch (start us, length us, event | category | flops | bytes accessed | tf_op | source)
XLA Modules:
  0.0 69.0 jit_solution(2368527117653088268)
XLA Ops:
  0.7 66.9 %imaging.1 = f32[16,512]{1,0:T(8,128)} custom-call(f32[1,16,512]{2,1,0:T(8,128)} %slow_ref.1, f32[1,16,512]{2,1,0:T(8,128)} %corr_ref.1, bf16[2,2,16,512]{3,2,1,0:T(8,128)(2,1)} %src_ref.1, bf16[2,2,16,512]{3,2,1,0:T(8,128)(2,1)} %adj_ref.1, f32[1]{0:T(128)S(6)} %copy.8.ref_ref, f32[2]{0:T(128)} %omega_ref.1), custom_call_target="tpu_custom_call" | custom-call | tf_op jit(solution)/shard_map/imaging/pallas_call | solution.py:759
  67.6 1.4 %copy.9 = f32[1,16,512]{2,1,0:T(8,128)} copy(f32[1,16,512]{2,1,0:T(8,128)} %bitcast.1) | data formatting | bytes 65536
